TPU v7x, 128 devices: a whole 4x4x4 slice. The times are simulated.
128 devices in a mesh: mic: 8 (over x_lo, z), tm: 16 (over x_hi, y, core).
Axes of the slice: x: 4 (x_hi: 2, x_lo: 2; x = x_hi * 2 + x_lo), y: 4, z: 4, core: 2. Of those that a mesh axis runs over, the one named last changes fastest.
Arguments:
- signal: float32 [8, 16384, 512], P('mic', 'tm'), may hold values from -6 to 6
- conv_weight: float32 [2, 3, 2, 512, 512], replicated, may hold values from -0.1875 to 0.1875
- conv_bias: float32 [2, 3, 512], replicated, may hold values from -3 to 3
- transform_in: float32 [2, 512, 512], replicated, may hold values from -0.25 to 0.25
- transform_mid: float32 [2, 512, 512], replicated, may hold values from -0.25 to 0.25
- transform_out: float32 [2, 1024, 512], replicated, may hold values from -0.1875 to 0.1875
- transform_offsets_bias: float32 [2, 3, 512], replicated, may hold values from -3 to 3
Outputs:
- separated: float32 [8, 16384, 512], P('mic', 'tm')
All inputs are finite; a program needn't handle non-finite values.
Results may differ from a plain program's by a relative error of at most 0.0001.
Values sent between devices are 32-bit elements; how exact they have to be, the bound alone decides.
No kernel may reach another device: no remote copies, remote signals or barrier semaphores. Data moves between devices by JAX's collectives and lax.ppermute only.
A program may use at most 128 MiB of HBM per device.

v0:
```python
import jax
import jax.numpy as jnp
from jax import lax
from jax.sharding import PartitionSpec as P

SEPARATOR_BLOCKS = 2


def from_behind(x, axis, by):
    length = lax.axis_size(axis)
    pairs = [(i, i + by) for i in range(length) if 0 <= i + by < length]
    return lax.ppermute(x, axis, pairs)


def matmul(left, right):
    return jnp.dot(left, right, precision=lax.Precision.HIGHEST, preferred_element_type=jnp.float32)


def convolve(hidden_activations, weights, bias, delayed):
    return hidden_activations + jnp.tanh(
        matmul(hidden_activations, weights[0]) + matmul(delayed, weights[1]) + bias
    )


def body(
    signal,
    conv_weight,
    conv_bias,
    transform_in,
    transform_mid,
    transform_out,
    transform_offsets_bias,
):
    hidden_activations = signal[0]
    frames = hidden_activations.shape[0]
    half = frames // 2
    channels = hidden_activations.shape[1]
    micro_count = jnp.float32(lax.axis_size("mic") * signal.shape[0])
    for section_index in range(SEPARATOR_BLOCKS):
        earlier = from_behind(hidden_activations, "tm", 1)[frames - half :]
        delayed = jnp.concatenate([earlier, hidden_activations[: frames - half]], axis=0)
        hidden_activations = convolve(
            hidden_activations, conv_weight[section_index, 0], conv_bias[section_index, 0], delayed
        )
        delayed = from_behind(hidden_activations, "tm", 1)
        hidden_activations = convolve(
            hidden_activations, conv_weight[section_index, 1], conv_bias[section_index, 1], delayed
        )
        delayed = from_behind(hidden_activations, "tm", 2)
        hidden_activations = convolve(
            hidden_activations, conv_weight[section_index, 2], conv_bias[section_index, 2], delayed
        )
        mapped = jnp.tanh(
            matmul(hidden_activations, transform_in[section_index])
            + transform_offsets_bias[section_index, 0]
        )
        summed = lax.psum(mapped, "mic")
        pooled = jnp.tanh(
            matmul(summed / micro_count, transform_mid[section_index])
            + transform_offsets_bias[section_index, 1]
        )
        mixing = (
            matmul(mapped, transform_out[section_index, :channels])
            + matmul(pooled, transform_out[section_index, channels:])
            + transform_offsets_bias[section_index, 2]
        )
        hidden_activations = hidden_activations + jnp.tanh(mixing)
    return hidden_activations[None]


def solution(mesh):
    placed = (P("mic", "tm", None), P(), P(), P(), P(), P(), P())
    return jax.shard_map(
        body, mesh=mesh, in_specs=placed, out_specs=P("mic", "tm", None), check_vma=False
    )
```

profile of v0, /device:TPU:1, one launch (start us, length us, event | category | flops | bytes accessed | tf_op | source)
XLA Modules:
  0.0 459.4 jit_solution(18367661636955650479)
XLA Ops:
  6.5 0.0 all-reduce.3.cloned.1.call-start
  6.5 4.7 %collective-permute-start = (f32[1024,512]{1,0:T(8,128)}, f32[1024,512]{1,0:T(8,128)S(1)}, u32[]{:S(2)}, u32[]{:S(2)}) collective-permute-start(f32[1024,512]{1,0:T(8,128)} %bitcast.93), channel_id=1, source_target_pairs={{0,1},{1,2},{2,3},{3,4},{4,5},{5,6},{6,7},{7,8},{8,9},{9,10},{10,1... | collective-permute-start | bytes 6291464 | tf_op jit(solution)/shard_map/ppermute | solution.py:12
  11.3 0.8 fusion.78
  12.0 1.3 slice_bitcast_fusion
  13.3 0.0 copy-done.2
  13.3 4.7 %fusion.46 = f32[1024,512]{1,0:T(8,128)S(1)} fusion(f32[2,3,2,512,512]{4,3,2,1,0:T(8,128)} %param.8, f32[1,1024,512]{2,1,0:T(8,128)S(1)} %copy-done.2), kind=kOutput, calls=%fused_computation.52 | convolution fusion | flops 3221225472 | bytes 5242880 | tf_op jit(solution)/shard_map/dot_general | solution.py:16
  18.0 16.5 %collective-permute-done = f32[1024,512]{1,0:T(8,128)S(1)} collective-permute-done((f32[1024,512]{1,0:T(8,128)}, f32[1024,512]{1,0:T(8,128)S(1)}, u32[]{:S(2)}, u32[]{:S(2)}) %collective-permute-start) | collective-permute-done | bytes 2097184 | tf_op jit(solution)/shard_map/ppermute | solution.py:12
  34.5 0.1 slice.178
  34.6 4.9 %tanh_add_fusion.6 = f32[1024,512]{1,0:T(8,128)S(1)} fusion(f32[1024,512]{1,0:T(8,128)S(1)} %fusion.46, f32[512,512]{1,0:T(8,128)S(1)} %slice_bitcast_fusion, f32[512,512]{1,0:T(8,128)S(1)} %slice.178, f32[512]{0:T(512)S(1)} %bitcast.105, f32[2,3,2,512,512]{4,3,2,1,0:T(8,128)} %param.8, f32[1,1024,512]{2,1,0:T(8,128)S(1)} %copy-done.2), kind=kOutput, calls=%fused_computation.27 | convolution fusion | flops 3223322624 | bytes 9439232 | tf_op jit(solution)/shard_map/dot_general | solution.py:16
  39.5 4.5 collective-permute-start.1
  44.0 4.7 %fusion.43 = f32[1024,512]{1,0:T(8,128)S(1)} fusion(f32[1024,512]{1,0:T(8,128)S(1)} %tanh_add_fusion.6, f32[2,3,2,512,512]{4,3,2,1,0:T(8,128)} %param.8), kind=kOutput, calls=%fused_computation.49 | convolution fusion | flops 3221225472 | bytes 5242880 | tf_op jit(solution)/shard_map/dot_general | solution.py:16
  48.7 18.0 %collective-permute-done.1 = f32[1024,512]{1,0:T(8,128)S(1)} collective-permute-done((f32[1024,512]{1,0:T(8,128)S(1)}, f32[1024,512]{1,0:T(8,128)S(1)}, u32[]{:S(2)}, u32[]{:S(2)}) %collective-permute-start.1) | collective-permute-done | bytes 2097184 | tf_op jit(solution)/shard_map/ppermute | solution.py:12
  66.8 5.0 %tanh_add_fusion.5 = f32[1024,512]{1,0:T(8,128)S(1)} fusion(f32[1024,512]{1,0:T(8,128)S(1)} %tanh_add_fusion.6, f32[1024,512]{1,0:T(8,128)S(1)} %fusion.43, f32[1024,512]{1,0:T(8,128)S(1)} %collective-permute-done.1, f32[512]{0:T(512)S(1)} %bitcast.103, f32[2,3,2,512,512]{4,3,2,1,0:T(8,128)} %param.8), kind=kOutput, calls=%fused_computation.26 | convolution fusion | flops 3222798336 | bytes 9439232 | tf_op jit(solution)/shard_map/dot_general | solution.py:16
  71.8 3.6 collective-permute-start.2
  75.3 0.0 copy-done.7
  75.4 4.7 %fusion.40 = f32[1024,512]{1,0:T(8,128)S(1)} fusion(f32[1024,512]{1,0:T(8,128)S(1)} %tanh_add_fusion.5, f32[2,3,2,512,512]{4,3,2,1,0:T(8,128)} %param.8), kind=kOutput, calls=%fused_computation.46 | convolution fusion | flops 3221225472 | bytes 5242880 | tf_op jit(solution)/shard_map/dot_general | solution.py:16
  80.1 38.5 %collective-permute-done.2 = f32[1024,512]{1,0:T(8,128)S(1)} collective-permute-done((f32[1024,512]{1,0:T(8,128)S(1)}, f32[1024,512]{1,0:T(8,128)S(1)}, u32[]{:S(2)}, u32[]{:S(2)}) %collective-permute-start.2) | collective-permute-done | bytes 2097184 | tf_op jit(solution)/shard_map/ppermute | solution.py:12
  118.6 5.1 %tanh_add_fusion.4 = f32[1024,512]{1,0:T(8,128)S(1)} fusion(f32[1024,512]{1,0:T(8,128)S(1)} %tanh_add_fusion.5, f32[1024,512]{1,0:T(8,128)S(1)} %fusion.40, f32[1024,512]{1,0:T(8,128)S(1)} %collective-permute-done.2, f32[512]{0:T(512)S(1)} %bitcast.100, f32[2,3,2,512,512]{4,3,2,1,0:T(8,128)} %param.8), kind=kOutput, calls=%fused_computation.25 | convolution fusion | flops 3222798336 | bytes 9439232 | tf_op jit(solution)/shard_map/dot_general | solution.py:16
  123.7 4.8 %add_tanh_fusion.1 = f32[1024,512]{1,0:T(8,128)} fusion(f32[1024,512]{1,0:T(8,128)S(1)} %tanh_add_fusion.4, f32[512]{0:T(512)S(1)} %bitcast.104, f32[2,512,512]{2,1,0:T(8,128)S(1)} %copy-done.5), kind=kOutput, calls=%fused_computation.24 | convolution fusion | flops 3221749760 | bytes 5244928 | tf_op jit(solution)/shard_map/dot_general | solution.py:16
  128.5 0.0 all-reduce.3.cloned.1.call-update
  128.5 0.5 all-reduce.5.cloned.1.call-start
  129.0 86.5 %all-reduce.3.cloned.1.call-done = f32[1024,512]{1,0:T(8,128)} async-done(((f32[1024,512]{1,0:T(8,128)}), f32[1024,512]{1,0:T(8,128)}) %all-reduce.3.cloned.1.call-update) | async-done | bytes 2097168 | tf_op jit(solution)/shard_map/psum | solution.py:57
  215.6 5.5 %fusion.16 = f32[1024,512]{1,0:T(8,128)S(1)} fusion(f32[1024,512]{1,0:T(8,128)} %all-reduce.3.cloned.1.call-done, f32[2,512,512]{2,1,0:T(8,128)} %param.11), kind=kOutput, calls=%fused_computation.22 | convolution fusion | flops 3221749760 | bytes 5242880 | tf_op jit(solution)/shard_map/dot_general | solution.py:16
  221.1 0.0 copy-start
  221.1 3.6 fusion.13
  224.6 0.0 copy-done
  224.7 3.7 tanh_add_fusion.3
  228.4 7.5 %collective-permute-start.3 = (f32[1024,512]{1,0:T(8,128)S(1)}, f32[1024,512]{1,0:T(8,128)S(1)}, u32[]{:S(2)}, u32[]{:S(2)}) collective-permute-start(f32[1024,512]{1,0:T(8,128)S(1)} %tanh_add_fusion.3), channel_id=1, source_target_pairs={{0,1},{1,2},{2,3},{3,4},{4,5},{5,6},{6,7},{7,8},{8,9},{9,10},{10,1... | collective-permute-start | bytes 6291464 | tf_op jit(solution)/shard_map/ppermute | solution.py:12
  235.9 0.1 slice.180
  236.0 4.7 %fusion.33 = f32[1024,512]{1,0:T(8,128)S(1)} fusion(f32[1024,512]{1,0:T(8,128)S(1)} %tanh_add_fusion.3, f32[2,3,2,512,512]{4,3,2,1,0:T(8,128)} %param.8), kind=kOutput, calls=%fused_computation.39 | convolution fusion | flops 3221225472 | bytes 5242880 | tf_op jit(solution)/shard_map/dot_general | solution.py:16
  240.7 18.0 %collective-permute-done.3 = f32[1024,512]{1,0:T(8,128)S(1)} collective-permute-done((f32[1024,512]{1,0:T(8,128)S(1)}, f32[1024,512]{1,0:T(8,128)S(1)}, u32[]{:S(2)}, u32[]{:S(2)}) %collective-permute-start.3) | collective-permute-done | bytes 2097184 | tf_op jit(solution)/shard_map/ppermute | solution.py:12
  258.7 0.1 slice.179
  258.8 5.0 %tanh_add_fusion.2 = f32[1024,512]{1,0:T(8,128)S(1)} fusion(f32[1024,512]{1,0:T(8,128)S(1)} %tanh_add_fusion.3, f32[1024,512]{1,0:T(8,128)S(1)} %fusion.33, f32[512,512]{1,0:T(8,128)S(1)} %slice.180, f32[512,512]{1,0:T(8,128)S(1)} %slice.179, f32[512]{0:T(512)S(1)} %bitcast.98, f32[2,3,2,512,512]{4,3,2,1,0:T(8,128)} %param.8), kind=kOutput, calls=%fused_computation.17 | convolution fusion | flops 3223322624 | bytes 9439232 | tf_op jit(solution)/shard_map/dot_general | solution.py:16
  263.7 4.4 collective-permute-start.4
  268.1 4.7 %fusion.30 = f32[1024,512]{1,0:T(8,128)S(1)} fusion(f32[1024,512]{1,0:T(8,128)S(1)} %tanh_add_fusion.2, f32[2,3,2,512,512]{4,3,2,1,0:T(8,128)} %param.8), kind=kOutput, calls=%fused_computation.36 | convolution fusion | flops 3221225472 | bytes 5242880 | tf_op jit(solution)/shard_map/dot_general | solution.py:16
  272.8 18.3 %collective-permute-done.4 = f32[1024,512]{1,0:T(8,128)S(1)} collective-permute-done((f32[1024,512]{1,0:T(8,128)S(1)}, f32[1024,512]{1,0:T(8,128)S(1)}, u32[]{:S(2)}, u32[]{:S(2)}) %collective-permute-start.4) | collective-permute-done | bytes 2097184 | tf_op jit(solution)/shard_map/ppermute | solution.py:12
  291.1 4.9 %tanh_add_fusion.1 = f32[1024,512]{1,0:T(8,128)S(1)} fusion(f32[1024,512]{1,0:T(8,128)S(1)} %tanh_add_fusion.2, f32[1024,512]{1,0:T(8,128)S(1)} %fusion.30, f32[1024,512]{1,0:T(8,128)S(1)} %collective-permute-done.4, f32[512]{0:T(512)S(1)} %bitcast.95, f32[2,3,2,512,512]{4,3,2,1,0:T(8,128)} %param.8), kind=kOutput, calls=%fused_computation.16 | convolution fusion | flops 3222798336 | bytes 9439232 | tf_op jit(solution)/shard_map/dot_general | solution.py:16
  296.0 3.5 collective-permute-start.5
  299.5 4.7 %fusion.27 = f32[1024,512]{1,0:T(8,128)S(1)} fusion(f32[1024,512]{1,0:T(8,128)S(1)} %tanh_add_fusion.1, f32[2,3,2,512,512]{4,3,2,1,0:T(8,128)} %param.8), kind=kOutput, calls=%fused_computation.33 | convolution fusion | flops 3221225472 | bytes 5242880 | tf_op jit(solution)/shard_map/dot_general | solution.py:16
  304.2 38.5 %collective-permute-done.5 = f32[1024,512]{1,0:T(8,128)S(1)} collective-permute-done((f32[1024,512]{1,0:T(8,128)S(1)}, f32[1024,512]{1,0:T(8,128)S(1)}, u32[]{:S(2)}, u32[]{:S(2)}) %collective-permute-start.5) | collective-permute-done | bytes 2097184 | tf_op jit(solution)/shard_map/ppermute | solution.py:12
  342.7 5.1 %tanh_add_fusion = f32[1024,512]{1,0:T(8,128)S(1)} fusion(f32[1024,512]{1,0:T(8,128)S(1)} %tanh_add_fusion.1, f32[1024,512]{1,0:T(8,128)S(1)} %fusion.27, f32[1024,512]{1,0:T(8,128)S(1)} %collective-permute-done.5, f32[512]{0:T(512)S(1)} %bitcast.94, f32[2,3,2,512,512]{4,3,2,1,0:T(8,128)} %param.8), kind=kOutput, calls=%fused_computation.15 | convolution fusion | flops 3222798336 | bytes 9439232 | tf_op jit(solution)/shard_map/dot_general | solution.py:16
  347.8 4.8 %add_tanh_fusion = f32[1024,512]{1,0:T(8,128)} fusion(f32[1024,512]{1,0:T(8,128)S(1)} %tanh_add_fusion, f32[512]{0:T(512)S(1)} %bitcast.99, f32[2,512,512]{2,1,0:T(8,128)S(1)} %copy-done.6), kind=kOutput, calls=%fused_computation.14 | convolution fusion | flops 3221749760 | bytes 5244928 | tf_op jit(solution)/shard_map/dot_general | solution.py:16
  352.6 0.0 all-reduce.5.cloned.1.call-update
  352.6 85.2 %all-reduce.5.cloned.1.call-done = f32[1024,512]{1,0:T(8,128)} async-done(((f32[1024,512]{1,0:T(8,128)}), f32[1024,512]{1,0:T(8,128)}) %all-reduce.5.cloned.1.call-update) | async-done | bytes 2097168 | tf_op jit(solution)/shard_map/psum | solution.py:57
  437.8 5.7 %fusion.11 = f32[1024,512]{1,0:T(8,128)S(1)} fusion(f32[1024,512]{1,0:T(8,128)} %all-reduce.5.cloned.1.call-done, f32[2,512,512]{2,1,0:T(8,128)} %param.11), kind=kOutput, calls=%fused_computation.12 | convolution fusion | flops 3221749760 | bytes 5242880 | tf_op jit(solution)/shard_map/dot_general | solution.py:16
  443.6 0.0 copy-start.1
  443.6 3.5 fusion.8
  447.1 5.0 %add_bitcast_fusion = f32[1,1024,512]{2,1,0:T(8,128)} fusion(f32[1024,512]{1,0:T(8,128)S(1)} %tanh_add_fusion, f32[1024,512]{1,0:T(8,128)S(1)} %fusion.8, f32[1024,512]{1,0:T(8,128)S(1)} %copy-done.1, f32[512]{0:T(512)S(1)} %bitcast.96, f32[2,1024,512]{2,1,0:T(8,128)S(1)} %copy-done.4), kind=kOutput, calls=%fused_computation.8 | convolution fusion | flops 3222798336 | bytes 9439232 | tf_op jit(solution)/shard_map/dot_general | solution.py:16
  (12 shorter events, 0.0 us)
Async XLA Ops:
  6.5 6.8 %copy-start.2 = (f32[1,1024,512]{2,1,0:T(8,128)S(1)}, f32[1,1024,512]{2,1,0:T(8,128)}, u32[]{:S(2)}) copy-start(f32[1,1024,512]{2,1,0:T(8,128)} %param.7) | copy-start | bytes 6291460
  6.5 209.0 %all-reduce.3.cloned.1.call-start = ((), (), s32[]{:S(2)}) async-start(), calls=%async_computation | async-start | bytes 4194304 | tf_op jit(solution)/shard_map/psum | solution.py:57
  6.5 28.0 %collective-permute-start = (f32[1024,512]{1,0:T(8,128)}, f32[1024,512]{1,0:T(8,128)S(1)}, u32[]{:S(2)}, u32[]{:S(2)}) collective-permute-start(f32[1024,512]{1,0:T(8,128)} %bitcast.93), channel_id=1, source_target_pairs={{0,1},{1,2},{2,3},{3,4},{4,5},{5,6},{6,7},{7,8},{8,9},{9,10},{10,1... | collective-permute-start | bytes 6291464 | tf_op jit(solution)/shard_map/ppermute | solution.py:12
  39.5 27.3 %collective-permute-start.1 = (f32[1024,512]{1,0:T(8,128)S(1)}, f32[1024,512]{1,0:T(8,128)S(1)}, u32[]{:S(2)}, u32[]{:S(2)}) collective-permute-start(f32[1024,512]{1,0:T(8,128)S(1)} %tanh_add_fusion.6), channel_id=1, source_target_pairs={{0,1},{1,2},{2,3},{3,4},{4,5},{5,6},{6,7},{7,8},{8,9},{9,10},{10,1... | collective-permute-start | bytes 6291464 | tf_op jit(solution)/shard_map/ppermute | solution.py:12
  66.8 8.6 %copy-start.7 = (f32[2,3,512]{2,0,1:T(2,128)S(1)}, f32[2,3,512]{2,0,1:T(2,128)}, u32[]{:S(2)}) copy-start(f32[2,3,512]{2,0,1:T(2,128)} %param.13) | copy-start | bytes 36868
  71.8 46.9 %collective-permute-start.2 = (f32[1024,512]{1,0:T(8,128)S(1)}, f32[1024,512]{1,0:T(8,128)S(1)}, u32[]{:S(2)}, u32[]{:S(2)}) collective-permute-start(f32[1024,512]{1,0:T(8,128)S(1)} %tanh_add_fusion.5), channel_id=1, source_target_pairs={{0,2},{1,3},{2,4},{3,5},{4,6},{5,7},{6,8},{7,9},{8,10},{9,11},{10,... | collective-permute-start | bytes 6291464 | tf_op jit(solution)/shard_map/ppermute | solution.py:12
  118.6 5.1 %copy-start.5 = (f32[2,512,512]{2,1,0:T(8,128)S(1)}, f32[2,512,512]{2,1,0:T(8,128)}, u32[]{:S(2)}) copy-start(f32[2,512,512]{2,1,0:T(8,128)} %param.10) | copy-start | bytes 6291460
  128.5 309.3 %all-reduce.5.cloned.1.call-start = ((), (), s32[]{:S(2)}) async-start(), calls=%async_computation.1 | async-start | bytes 4194304 | tf_op jit(solution)/shard_map/psum | solution.py:57
  215.6 5.5 %copy-start.3 = (f32[2,1024,512]{2,1,0:T(8,128)S(1)}, f32[2,1024,512]{2,1,0:T(8,128)}, u32[]{:S(2)}) copy-start(f32[2,1024,512]{2,1,0:T(8,128)} %param.12) | copy-start | bytes 12582916
  221.1 3.6 copy-start
  228.4 30.3 %collective-permute-start.3 = (f32[1024,512]{1,0:T(8,128)S(1)}, f32[1024,512]{1,0:T(8,128)S(1)}, u32[]{:S(2)}, u32[]{:S(2)}) collective-permute-start(f32[1024,512]{1,0:T(8,128)S(1)} %tanh_add_fusion.3), channel_id=1, source_target_pairs={{0,1},{1,2},{2,3},{3,4},{4,5},{5,6},{6,7},{7,8},{8,9},{9,10},{10,1... | collective-permute-start | bytes 6291464 | tf_op jit(solution)/shard_map/ppermute | solution.py:12
  263.7 27.4 %collective-permute-start.4 = (f32[1024,512]{1,0:T(8,128)S(1)}, f32[1024,512]{1,0:T(8,128)S(1)}, u32[]{:S(2)}, u32[]{:S(2)}) collective-permute-start(f32[1024,512]{1,0:T(8,128)S(1)} %tanh_add_fusion.2), channel_id=1, source_target_pairs={{0,1},{1,2},{2,3},{3,4},{4,5},{5,6},{6,7},{7,8},{8,9},{9,10},{10,1... | collective-permute-start | bytes 6291464 | tf_op jit(solution)/shard_map/ppermute | solution.py:12
  296.0 46.7 %collective-permute-start.5 = (f32[1024,512]{1,0:T(8,128)S(1)}, f32[1024,512]{1,0:T(8,128)S(1)}, u32[]{:S(2)}, u32[]{:S(2)}) collective-permute-start(f32[1024,512]{1,0:T(8,128)S(1)} %tanh_add_fusion.1), channel_id=1, source_target_pairs={{0,2},{1,3},{2,4},{3,5},{4,6},{5,7},{6,8},{7,9},{8,10},{9,11},{10,... | collective-permute-start | bytes 6291464 | tf_op jit(solution)/shard_map/ppermute | solution.py:12
  342.7 5.1 %copy-start.6 = (f32[2,512,512]{2,1,0:T(8,128)S(1)}, f32[2,512,512]{2,1,0:T(8,128)}, u32[]{:S(2)}) copy-start(f32[2,512,512]{2,1,0:T(8,128)} %param.10) | copy-start | bytes 6291460
  437.8 5.8 %copy-start.4 = (f32[2,1024,512]{2,1,0:T(8,128)S(1)}, f32[2,1024,512]{2,1,0:T(8,128)}, u32[]{:S(2)}) copy-start(f32[2,1024,512]{2,1,0:T(8,128)} %param.12) | copy-start | bytes 12582916
  443.6 3.5 copy-start.1
Sparse Core Ops, SparseCore 0:
  128.6 86.8 all-reduce.2
  352.7 85.0 all-reduce.4
where the time goes:
time: 469 us; the launch traced here: 459 us
  waiting for transfers between devices  320 us (68%)
  matrix products  94.6 us (20%)
  starting transfers between devices  28.7 us (6%)
  between operations  14.1 us (3%)
    psum x2, waiting for transfers between devices, body(): summed = lax.psum(mapped, 'mic')  172 us
    ppermute x6, waiting for transfers between devices, from_behind(): return lax.ppermute(x, axis, pairs)  148 us
    dot_general x20, matrix products, matmul(): jnp.dot(left, right, precision=lax.Precision.HIGHEST, preferred_element_t...  94.6 us
    ppermute x6, starting transfers between devices, from_behind(): return lax.ppermute(x, axis, pairs)  28.2 us
  transfers between devices with their start and end apart: 8, of which 8 were waited for; matrix products, arithmetic and copies ran while one was open for 7% of the time, Pallas kernels for 0%

commit v1 on v0

v1 whole, which is shorter than its diff:
```python
import functools

import jax
import jax.numpy as jnp
from jax import lax
from jax.experimental import pallas as pl
from jax.experimental.pallas import tpu as pltpu
from jax.sharding import PartitionSpec as P

SECTIONS = 2
LAYERS = 3
BASE = 512
MICS = 8
LANES = 512
TILE = 8
COLS = 128
CHUNKS = 2
F32 = jnp.float32
BF16 = jnp.bfloat16
BOTH = ("mic", "tm")
VMEM = pl.BlockSpec(memory_space=pltpu.VMEM)
ANY = pl.BlockSpec(memory_space=pl.ANY)


def halves(x):
    hi = x.astype(BF16)
    lo = (x - hi.astype(F32)).astype(BF16)
    return hi, lo


def pack_kernel(chunk, x_ref, out_ref):
    rows = TILE // CHUNKS
    groups = LANES // COLS
    for k in range(rows):
        start = 128 * (chunk + CHUNKS * k)
        for g in range(groups):
            out_ref[pl.ds(g * rows + k, 128, stride=groups * rows), :] = x_ref[
                start : start + 128, g * COLS : (g + 1) * COLS
            ]


def unpack_kernel(*refs):
    y_refs, out_ref = refs[:-1], refs[-1]
    rows = TILE // CHUNKS
    groups = LANES // COLS
    for chunk, y_ref in enumerate(y_refs):
        for k in range(rows):
            start = 128 * (chunk + CHUNKS * k)
            for g in range(groups):
                out_ref[start : start + 128, g * COLS : (g + 1) * COLS] = y_ref[
                    pl.ds(g * rows + k, 128, stride=groups * rows), :
                ]


def split_kernel(*refs):
    n = len(refs) // 3
    for i in range(n):
        hi, lo = halves(refs[i][...])
        refs[n + 2 * i][...] = hi
        refs[n + 2 * i + 1][...] = lo


def split_weights(arrays):
    steps = 8
    specs = [pl.BlockSpec((a.shape[0] // steps, a.shape[1]), lambda i: (i, 0)) for a in arrays]
    size = sum(a.size for a in arrays)
    return pl.pallas_call(
        split_kernel,
        grid=(steps,),
        in_specs=specs,
        out_specs=[s for s in specs for _ in range(2)],
        out_shape=[jax.ShapeDtypeStruct(a.shape, BF16) for a in arrays for _ in range(2)],
        cost_estimate=pl.CostEstimate(flops=4 * size, bytes_accessed=8 * size, transcendentals=0),
        name="split_weights",
    )(*arrays)


def dot3(ahi, alo, whi, wlo):
    dot = functools.partial(jnp.dot, preferred_element_type=F32)
    return dot(ahi, whi) + dot(ahi, wlo) + dot(alo, whi)


def network_kernel(per, block, x_ref, cb_ref, tb_ref, *refs):
    (c_hi, c_lo, i_hi, i_lo, m_hi, m_lo, o_hi, o_lo, out_ref) = refs[:9]
    (h_ref, a_hi, a_lo, u_ref, u_hi, u_lo, p_ref) = refs[9:16]
    (wc_hi, wc_lo, wi_hi, wi_lo, wm_hi, wm_lo, wo_hi, wo_lo, sems) = refs[16:]
    rows, width = h_ref.shape
    step = per * MICS
    pad = a_hi.shape[1] - rows
    quotients = rows // step
    groups = width // COLS
    piece = 2 * per * groups

    def copies(s):
        out = []
        for l in range(LAYERS):
            k = s * LAYERS + l
            out += [(c_hi.at[k], wc_hi.at[k], sems.at[s, 2 * l]), (c_lo.at[k], wc_lo.at[k], sems.at[s, 2 * l + 1])]
        for j, (src, dst) in enumerate(
            [(i_hi, wi_hi), (i_lo, wi_lo), (m_hi, wm_hi), (m_lo, wm_lo), (o_hi, wo_hi), (o_lo, wo_lo)]
        ):
            out.append((src.at[s], dst.at[s], sems.at[s, 2 * LAYERS + j]))
        return [pltpu.make_async_copy(*c) for c in out]

    for s in range(SECTIONS):
        for c in copies(s):
            c.start()

    for slot in range(2):
        a_hi[slot, 0:pad, :] = jnp.zeros((pad, width), BF16)
        a_lo[slot, 0:pad, :] = jnp.zeros((pad, width), BF16)

    tms = x_ref.shape[0] // piece // MICS
    for tm in range(tms):
        for qp in range(2):
            for r in range(per):
                row = ((2 * tm + qp) * per + r) * MICS
                for g in range(groups):
                    h_ref[row : row + MICS, g * COLS : (g + 1) * COLS] = x_ref[
                        pl.ds(tm * piece + (g * 2 + qp) * per + r, MICS, stride=tms * piece), :
                    ]

    blocks = rows // block

    def put(slot, start, h):
        hi, lo = halves(h)
        a_hi[slot, pl.ds(pad + start, block), :] = hi
        a_lo[slot, pl.ds(pad + start, block), :] = lo

    def first(b, _):
        start = pl.multiple_of(b * block, block)
        put(0, start, h_ref[pl.ds(start, block), :])
        return 0

    lax.fori_loop(0, blocks, first, 0)

    def section(s, _):
        def layer(l, _):
            k = s * LAYERS + l
            cur = lax.rem(l, 2)
            shift = pl.multiple_of(step * lax.shift_left(1, l), step)
            pltpu.make_async_copy(c_hi.at[k], wc_hi.at[k], sems.at[s, 2 * l]).wait()
            pltpu.make_async_copy(c_lo.at[k], wc_lo.at[k], sems.at[s, 2 * l + 1]).wait()

            def one(b, _):
                start = pl.multiple_of(b * block, block)
                here = pl.ds(pad + start, block)
                past = pl.ds(pl.multiple_of(pad + start - shift, step), block)
                pre = dot3(a_hi[cur, here, :], a_lo[cur, here, :], wc_hi[k, :width, :], wc_lo[k, :width, :])
                pre += dot3(a_hi[cur, past, :], a_lo[cur, past, :], wc_hi[k, width:, :], wc_lo[k, width:, :])
                h = h_ref[pl.ds(start, block), :] + jnp.tanh(pre + cb_ref[pl.ds(k, 1), :])
                h_ref[pl.ds(start, block), :] = h
                put(1 - cur, start, h)
                return 0

            lax.fori_loop(0, blocks, one, 0)
            return 0

        lax.fori_loop(0, LAYERS, layer, 0)
        last = LAYERS % 2
        for j, (src, dst) in enumerate(
            [(i_hi, wi_hi), (i_lo, wi_lo), (m_hi, wm_hi), (m_lo, wm_lo), (o_hi, wo_hi), (o_lo, wo_lo)]
        ):
            pltpu.make_async_copy(src.at[s], dst.at[s], sems.at[s, 2 * LAYERS + j]).wait()

        def inner(b, _):
            start = pl.multiple_of(b * block, block)
            here = pl.ds(pad + start, block)
            pre = dot3(a_hi[last, here, :], a_lo[last, here, :], wi_hi[s], wi_lo[s])
            u = jnp.tanh(pre + tb_ref[pl.ds(3 * s, 1), :])
            for g in range(groups):
                u_ref[g, pl.ds(start, block), :] = u[:, g * COLS : (g + 1) * COLS]
            hi, lo = halves(u)
            u_hi[pl.ds(start, block), :] = hi
            u_lo[pl.ds(start, block), :] = lo
            return 0

        lax.fori_loop(0, blocks, inner, 0)

        frames = rows // MICS
        means = []
        for g in range(groups):
            total = u_ref[g, pl.ds(0, frames, stride=MICS), :]
            for m in range(1, MICS):
                total += u_ref[g, pl.ds(m, frames, stride=MICS), :]
            means.append(total * (1.0 / MICS))
        hi, lo = halves(jnp.concatenate(means, axis=1))
        v = jnp.tanh(dot3(hi, lo, wm_hi[s], wm_lo[s]) + tb_ref[pl.ds(3 * s + 1, 1), :])
        hi, lo = halves(v)
        p_ref[...] = dot3(hi, lo, wo_hi[s, width:, :], wo_lo[s, width:, :]) + tb_ref[pl.ds(3 * s + 2, 1), :]

        def outer(b, _):
            start = pl.multiple_of(b * block, block)
            here = pl.ds(start, block)
            pre = dot3(u_hi[here, :], u_lo[here, :], wo_hi[s, :width, :], wo_lo[s, :width, :])
            base = pl.multiple_of(b * (block // MICS), block // MICS)
            pooled = jnp.concatenate(
                [jnp.broadcast_to(p_ref[pl.ds(base + j, 1), :], (MICS, width)) for j in range(block // MICS)], axis=0
            )
            h = h_ref[here, :] + jnp.tanh(pre + pooled)
            h_ref[here, :] = h
            put(0, start, h)
            return 0

        lax.fori_loop(0, blocks, outer, 0)
        return 0

    lax.fori_loop(0, SECTIONS, section, 0)

    for tm in range(tms):
        for qp in range(2):
            for r in range(per):
                row = ((2 * tm + qp) * per + r) * MICS
                for g in range(groups):
                    out_ref[pl.ds(tm * piece + (g * 2 + qp) * per + r, MICS, stride=tms * piece), :] = h_ref[
                        row : row + MICS, g * COLS : (g + 1) * COLS
                    ]


def network(x, biases, weights, block=256):
    rows = x.size // LANES
    width = LANES
    per = rows // MICS // 32
    pad = 4 * per * MICS
    cb, tb = biases
    scratch = [
        pltpu.VMEM((rows, width), F32),
        pltpu.VMEM((2, pad + rows, width), BF16),
        pltpu.VMEM((2, pad + rows, width), BF16),
        pltpu.VMEM((width // COLS, rows, COLS), F32),
        pltpu.VMEM((rows, width), BF16),
        pltpu.VMEM((rows, width), BF16),
        pltpu.VMEM((rows // MICS, width), F32),
    ]
    scratch += [pltpu.VMEM(w.shape, BF16) for w in weights]
    scratch += [pltpu.SemaphoreType.DMA((SECTIONS, 2 * LAYERS + 6))]
    flops = 2 * 3 * rows * width * width * (SECTIONS * (2 * LAYERS + 2)) + 2 * 3 * rows // MICS * width * width * 4
    return pl.pallas_call(
        functools.partial(network_kernel, per, block),
        in_specs=[VMEM] * 3 + [ANY] * len(weights),
        out_specs=VMEM,
        out_shape=jax.ShapeDtypeStruct(x.shape, F32),
        scratch_shapes=scratch,
        compiler_params=pltpu.CompilerParams(vmem_limit_bytes=48 << 20),
        cost_estimate=pl.CostEstimate(
            flops=flops, bytes_accessed=sum(2 * w.size for w in weights), transcendentals=rows * width * 10
        ),
        name="network",
    )(x, cb, tb, *weights)


def pack(x, chunk):
    return pl.pallas_call(
        functools.partial(pack_kernel, chunk),
        in_specs=[VMEM],
        out_specs=VMEM,
        out_shape=jax.ShapeDtypeStruct((x.size // CHUNKS // COLS, COLS), F32),
        name="pack",
    )(x)


def exchange(x):
    devices = lax.axis_size(BOTH)
    pieces = x.reshape(devices, x.shape[0] // devices, x.shape[1])
    return lax.all_to_all(pieces, BOTH, 0, 0, tiled=True).reshape(x.shape)


def body(signal, conv_weight, conv_bias, transform_in, transform_mid, transform_out, transform_offsets_bias):
    x = signal[0]
    width = x.shape[1]
    received = [exchange(pack(x, c)) for c in range(CHUNKS)]
    flat = [w.reshape(-1, width) for w in (conv_weight, transform_in, transform_mid, transform_out)]
    c_hi, c_lo, i_hi, i_lo, m_hi, m_lo, o_hi, o_lo = split_weights(flat)
    weights = [w.reshape(SECTIONS * LAYERS, 2 * width, width) for w in (c_hi, c_lo)]
    weights += [w.reshape(SECTIONS, width, width) for w in (i_hi, i_lo, m_hi, m_lo)]
    weights += [w.reshape(SECTIONS, 2 * width, width) for w in (o_hi, o_lo)]
    biases = conv_bias.reshape(-1, width), transform_offsets_bias.reshape(-1, width)
    back = [exchange(network(y, biases, weights)) for y in received]
    return pl.pallas_call(
        unpack_kernel,
        in_specs=[VMEM] * CHUNKS,
        out_specs=VMEM,
        out_shape=jax.ShapeDtypeStruct(x.shape, F32),
        name="unpack",
    )(*back)[None]


def solution(mesh):
    placed = (P("mic", "tm", None), P(), P(), P(), P(), P(), P())
    return jax.shard_map(body, mesh=mesh, in_specs=placed, out_specs=P("mic", "tm", None), check_vma=False)
```

time: 469 us -> 136 us (0.29); the launches traced: 459 us -> 135 us
  waiting for transfers between devices: 320 us -> 0.23 us
  matrix products: 94.6 us -> 0 us
  Pallas kernels: 0 us -> 69.6 us
  blocking collectives: 0 us -> 29.2 us
  between operations: 14.1 us -> 0.14 us
    psum x2 -> x0, waiting for transfers between devices: 172 us -> none  [body(): summed = lax.psum(mapped, 'mic')]
    ppermute x6 -> x0, waiting for transfers between devices: 148 us -> none  [from_behind(): return lax.ppermute(x, axis, pairs)]
    dot_general x20 -> x0, matrix products: 94.6 us -> none  [matmul(): jnp.dot(left, right, precision=lax.Precision.HIGHEST, preferred_element_t...]
    pallas_call x0 -> x6, Pallas kernels: none -> 69.6 us  [the longest x2 43.8 us: network(): pl.pallas_call(functools.partial(network_kernel, per, block), in_specs=[V...]
    all_to_all x0 -> x3, starting transfers between devices: none -> 31.3 us  [exchange(): return lax.all_to_all(pieces, BOTH, 0, 0, tiled=True).reshape(x.shape)]
    all_to_all x0 -> x1, blocking collectives: none -> 29.2 us  [exchange(): return lax.all_to_all(pieces, BOTH, 0, 0, tiled=True).reshape(x.shape)]
    ppermute x6 -> x0, starting transfers between devices: 28.2 us -> none  [from_behind(): return lax.ppermute(x, axis, pairs)]
    unnamed x16, local copies, waits for them, and re-layouts: 0.03 us -> 4.91 us
  transfers between devices with their start and end apart: 8 -> 3, of which waited for: 8 -> 1; matrix products, arithmetic and copies ran while one was open for 7% -> 0% of each run, Pallas kernels for 0% -> 47%
where the time goes in v1:
time: 136 us; the launch traced here: 135 us
  Pallas kernels  69.6 us (51%)
  starting transfers between devices  31.3 us (23%)
  blocking collectives  29.2 us (21%)
  local copies, waits for them, and re-layouts  4.93 us (4%)
    pallas_call x2, Pallas kernels, network(): pl.pallas_call(functools.partial(network_kernel, per, block), in_specs=[V...  43.8 us
    all_to_all x3, starting transfers between devices, exchange(): return lax.all_to_all(pieces, BOTH, 0, 0, tiled=True).reshape(x.shape)  31.3 us
    all_to_all x1, blocking collectives, exchange(): return lax.all_to_all(pieces, BOTH, 0, 0, tiled=True).reshape(x.shape)  29.2 us
    pallas_call x1, Pallas kernels, split_weights(): pl.pallas_call(split_kernel, grid=(steps,), in_specs=specs, out_specs=[s...  16.1 us
    pallas_call x2, Pallas kernels, pack(): pl.pallas_call(functools.partial(pack_kernel, chunk), in_specs=[VMEM], ou...  6.18 us
    unnamed x16, local copies, waits for them, and re-layouts  4.91 us
    pallas_call x1, Pallas kernels, body(): pl.pallas_call(unpack_kernel, in_specs=[VMEM] * CHUNKS, out_specs=VMEM, o...  3.52 us
  transfers between devices with their start and end apart: 3, of which 1 were waited for; matrix products, arithmetic and copies ran while one was open for 0% of the time, Pallas kernels for 47%

profile of v1, /device:TPU:1, one launch (start us, length us, event | category | flops | bytes accessed | tf_op | source)
XLA Modules:
  0.0 135.3 jit_solution(18444530947848109052)
XLA Ops:
  0.0 3.1 %pack.3 = f32[2048,128]{1,0:T(8,128)} custom-call(f32[1024,512]{1,0:T(8,128)} %bitcast.32), custom_call_target="tpu_custom_call" | custom-call | tf_op jit(solution)/shard_map/pack/pallas_call | solution.py:253
  3.1 11.5 %all-to-all-start.2 = ((f32[128,16,128]{2,1,0:T(8,128)}), f32[128,16,128]{2,1,0:T(8,128)S(1)}, u32[]{:S(2)}, u32[]{:S(2)}) async-start(f32[128,16,128]{2,1,0:T(8,128)} %bitcast.36), calls=%async_computation.2 | async-start | bytes 2097152 | tf_op jit(solution)/shard_map/all_to_all | solution.py:265
  14.6 0.0 copy-start.5
  14.6 0.0 copy-start.6
  14.6 3.1 %pack.2 = f32[2048,128]{1,0:T(8,128)} custom-call(f32[1024,512]{1,0:T(8,128)} %bitcast.33), custom_call_target="tpu_custom_call" | custom-call | tf_op jit(solution)/shard_map/pack/pallas_call | solution.py:253
  17.7 0.0 copy-done.5
  17.7 0.0 copy-done.6
  17.8 16.1 %split_weights.1 = (bf16[6144,512]{1,0:T(8,128)(2,1)}, bf16[6144,512]{1,0:T(8,128)(2,1)}, bf16[1024,512]{1,0:T(8,128)(2,1)}, bf16[1024,512]{1,0:T(8,128)(2,1)}, ...) custom-call(f32[6144,512]{1,0:T(8,128)} %bitcast.31, ...), custom_call_target="tpu_custom_call" | custom-call | flops 20971520 | bytes 41943040 | tf_op jit(solution)/shard_map/split_weights/pallas_call | solution.py:67
  33.8 0.0 copy-start
  33.8 0.2 all-to-all-done.2
  34.1 9.6 %all-to-all-start = ((f32[128,16,128]{2,1,0:T(8,128)}), f32[128,16,128]{2,1,0:T(8,128)S(1)}, u32[]{:S(2)}, u32[]{:S(2)}) async-start(f32[128,16,128]{2,1,0:T(8,128)} %bitcast.35), calls=%async_computation | async-start | bytes 2097152 | tf_op jit(solution)/shard_map/all_to_all | solution.py:265
  43.6 0.0 copy-done
  43.6 0.0 copy-start.1
  43.6 1.2 copy-done.1
  44.9 0.0 copy-start.3
  44.9 1.2 copy-done.3
  46.1 22.4 %network.3 = f32[2048,128]{1,0:T(8,128)} custom-call(f32[2048,128]{1,0:T(8,128)S(1)} %bitcast.22, f32[6,512]{1,0:T(8,128)S(1)} %reshape.68.cb_ref, f32[6,512]{1,0:T(8,128)S(1)} %reshape.69.tb_ref, bf16[6,1024,512]{2,1,0:T(8,128)(2,1)} %bitcast.40, bf16[6,1024,512]{2,1,0:T(8,128)(2,1)} %bitcast.42, bf16[2,512,512]{2,1,0:T(8,128)(2,1)S(1)} %bitcast.25, ...), custom_call_target="tpu_custom_call" | custom-call | flops 13287555072 | bytes 20971520 | tf_op jit(solution)/shard_map/network/pallas_call | solution.py:238
  68.5 0.0 all-to-all-done
  68.5 10.2 %all-to-all-start.3 = ((f32[128,16,128]{2,1,0:T(8,128)}), f32[128,16,128]{2,1,0:T(8,128)}, u32[]{:S(2)}, u32[]{:S(2)}) async-start(f32[128,16,128]{2,1,0:T(8,128)} %bitcast.19), calls=%async_computation.3 | async-start | bytes 2097152 | tf_op jit(solution)/shard_map/all_to_all | solution.py:265
  78.7 0.0 copy-start.2
  78.7 1.2 copy-done.2
  79.9 0.0 copy-start.4
  79.9 1.2 copy-done.4
  81.2 21.5 %network.2 = f32[2048,128]{1,0:T(8,128)S(1)} custom-call(f32[2048,128]{1,0:T(8,128)S(1)} %bitcast.23, f32[6,512]{1,0:T(8,128)S(1)} %reshape.68.cb_ref, f32[6,512]{1,0:T(8,128)S(1)} %reshape.69.tb_ref, bf16[6,1024,512]{2,1,0:T(8,128)(2,1)} %bitcast.41, bf16[6,1024,512]{2,1,0:T(8,128)(2,1)} %bitcast.43, bf16[2,512,512]{2,1,0:T(8,128)(2,1)S(1)} %bitcast.26, ...), custom_call_target="tpu_custom_call" | custom-call | flops 13287555072 | bytes 20971520 | tf_op jit(solution)/shard_map/network/pallas_call | solution.py:238
  102.6 0.0 all-to-all-done.3
  102.6 29.2 %all_to_all.20 = f32[128,16,128]{2,1,0:T(8,128)} all-to-all(f32[128,16,128]{2,1,0:T(8,128)S(1)} %bitcast.24), channel_id=1, replica_groups=mesh['mic'=8,'tm'=16] {'mic','tm'}, dimensions={0} | all-to-all | bytes 2097152 | tf_op jit(solution)/shard_map/all_to_all | solution.py:265
  131.8 3.5 %unpack.1 = f32[1024,512]{1,0:T(8,128)} custom-call(f32[2048,128]{1,0:T(8,128)} %bitcast.37, f32[2048,128]{1,0:T(8,128)} %bitcast.20.refs_1_), custom_call_target="tpu_custom_call" | custom-call | tf_op jit(solution)/shard_map/unpack/pallas_call | solution.py:279
  (4 shorter events, 0.0 us)
Async XLA Ops:
  3.1 31.0 %all-to-all-start.2 = ((f32[128,16,128]{2,1,0:T(8,128)}), f32[128,16,128]{2,1,0:T(8,128)S(1)}, u32[]{:S(2)}, u32[]{:S(2)}) async-start(f32[128,16,128]{2,1,0:T(8,128)} %bitcast.36), calls=%async_computation.2 | async-start | bytes 2097152 | tf_op jit(solution)/shard_map/all_to_all | solution.py:265
  14.6 3.1 %copy-start.5 = (f32[2,3,512]{2,0,1:T(2,128)S(1)}, f32[2,3,512]{2,0,1:T(2,128)}, u32[]{:S(2)}) copy-start(f32[2,3,512]{2,0,1:T(2,128)} %param.9) | copy-start | bytes 36868
  14.6 3.1 %copy-start.6 = (f32[2,3,512]{2,0,1:T(2,128)S(1)}, f32[2,3,512]{2,0,1:T(2,128)}, u32[]{:S(2)}) copy-start(f32[2,3,512]{2,0,1:T(2,128)} %param.13) | copy-start | bytes 36868
  33.8 9.8 %copy-start = (bf16[1024,512]{1,0:T(8,128)(2,1)S(1)}, bf16[1024,512]{1,0:T(8,128)(2,1)}, u32[]{:S(2)}) copy-start(bf16[1024,512]{1,0:T(8,128)(2,1)} %get-tuple-element.15) | copy-start | bytes 3145732
  34.1 34.4 %all-to-all-start = ((f32[128,16,128]{2,1,0:T(8,128)}), f32[128,16,128]{2,1,0:T(8,128)S(1)}, u32[]{:S(2)}, u32[]{:S(2)}) async-start(f32[128,16,128]{2,1,0:T(8,128)} %bitcast.35), calls=%async_computation | async-start | bytes 2097152 | tf_op jit(solution)/shard_map/all_to_all | solution.py:265
  43.6 1.2 copy-start.1
  44.9 1.2 copy-start.3
  68.5 34.2 %all-to-all-start.3 = ((f32[128,16,128]{2,1,0:T(8,128)}), f32[128,16,128]{2,1,0:T(8,128)}, u32[]{:S(2)}, u32[]{:S(2)}) async-start(f32[128,16,128]{2,1,0:T(8,128)} %bitcast.19), calls=%async_computation.3 | async-start | bytes 2097152 | tf_op jit(solution)/shard_map/all_to_all | solution.py:265
  78.7 1.2 copy-start.2
  79.9 1.2 copy-start.4

commit v2 on v0

v2 whole, which is shorter than its diff:
```python
import functools

import jax
import jax.numpy as jnp
from jax import lax
from jax.experimental import pallas as pl
from jax.experimental.pallas import tpu as pltpu
from jax.sharding import PartitionSpec as P

SECTIONS = 2
LAYERS = 3
MICS = 8
COLS = 128
GRANT = 65400 * 1024
F32 = jnp.float32
BF16 = jnp.bfloat16
BOTH = ("mic", "tm")
VMEM = pl.BlockSpec(memory_space=pltpu.VMEM)
ANY = pl.BlockSpec(memory_space=pl.ANY)
PARAMS = pltpu.CompilerParams(vmem_limit_bytes=GRANT)


def halves(x):
    hi = x.astype(BF16)
    lo = (x - hi.astype(F32)).astype(BF16)
    return hi, lo


def taps_kernel(w_ref, hi_ref, lo_ref):
    width = w_ref.shape[1]
    now, past = w_ref[:width, :], w_ref[width:, :]
    for i, w in enumerate((now, past, now + past)):
        part = slice(i * width, (i + 1) * width)
        hi_ref[part, :], lo_ref[part, :] = halves(w)


def split_taps(w):
    layers = SECTIONS * LAYERS
    rows, width = w.shape
    spec = pl.BlockSpec((rows // layers // 2 * 3, width), lambda i: (i, 0))
    out = jax.ShapeDtypeStruct((rows // 2 * 3, width), BF16)
    return pl.pallas_call(
        taps_kernel,
        grid=(layers,),
        in_specs=[pl.BlockSpec((rows // layers, width), lambda i: (i, 0))],
        out_specs=[spec] * 2,
        out_shape=[out] * 2,
        compiler_params=PARAMS,
        cost_estimate=pl.CostEstimate(flops=6 * w.size, bytes_accessed=10 * w.size, transcendentals=0),
        name="split_taps",
    )(w)


def dense_kernel(*refs):
    n = len(refs) // 3
    for i in range(n):
        refs[n + 2 * i][...], refs[n + 2 * i + 1][...] = halves(refs[i][...])


def split_dense(arrays, steps=4):
    specs = [pl.BlockSpec((a.shape[0] // steps, a.shape[1]), lambda i: (i, 0)) for a in arrays]
    size = sum(a.size for a in arrays)
    return pl.pallas_call(
        dense_kernel,
        grid=(steps,),
        in_specs=specs,
        out_specs=[p for p in specs for _ in range(2)],
        out_shape=[jax.ShapeDtypeStruct(a.shape, BF16) for a in arrays for _ in range(2)],
        compiler_params=PARAMS,
        cost_estimate=pl.CostEstimate(flops=4 * size, bytes_accessed=8 * size, transcendentals=0),
        name="split_dense",
    )(*arrays)


def dot3(a, w):
    dot = functools.partial(jnp.dot, preferred_element_type=F32)
    return dot(a[0], w[0]) + dot(a[0], w[1]) + dot(a[1], w[0])


def network_kernel(per, x_ref, cb_ref, tb_ref, *refs):
    n = 8
    sources, out_ref, h_ref, u_ref = refs[:n], *refs[n : n + 3]
    held, sems = refs[n + 3 : 2 * n + 3], refs[2 * n + 3]
    rows, width = h_ref.shape
    step = per * MICS
    groups = width // COLS
    piece = 2 * per * groups
    tms = x_ref.shape[0] // piece // MICS

    def fetch(j, k):
        size = held[j].shape[0] // (SECTIONS * LAYERS if j < 2 else SECTIONS)
        part = pl.ds(pl.multiple_of(k * size, size), size)
        return pltpu.make_async_copy(sources[j].at[part, :], held[j].at[part, :], sems.at[j, k])

    for s in range(SECTIONS):
        for l in range(LAYERS):
            for j in range(2):
                fetch(j, s * LAYERS + l).start()
        for j in range(2, n):
            fetch(j, s).start()

    def spots():
        for tm in range(tms):
            for qp in range(2):
                for r in range(per):
                    row = ((2 * tm + qp) * per + r) * MICS
                    for g in range(groups):
                        spot = pl.ds(tm * piece + (g * 2 + qp) * per + r, MICS, stride=tms * piece)
                        yield spot, slice(row, row + MICS), slice(g * COLS, (g + 1) * COLS)

    def weight(j, first):
        part = pl.ds(pl.multiple_of(first, width), width)
        return held[j][part, :], held[j + 1][part, :]

    def layer(s, l):
        k = s * LAYERS + l
        for j in range(2):
            fetch(j, k).wait()
        span = step * 2**l
        evens = [pl.ds(2 * p * span, span) for p in range(rows // span // 2)]
        odds = [pl.ds((2 * p + 1) * span, span) for p in range(rows // span // 2)]
        even = jnp.concatenate([h_ref[p, :] for p in evens], axis=0)
        odd = jnp.concatenate([h_ref[p, :] for p in odds], axis=0)
        past = jnp.concatenate([jnp.zeros((span, width), F32)] + [h_ref[p, :] for p in odds[:-1]], axis=0)
        first = 3 * k * width
        shared = dot3(halves(even), weight(0, first + 2 * width)) + cb_ref[s, l : l + 1, :]
        y_even = shared + dot3(halves(past - even), weight(0, first + width))
        y_odd = shared + dot3(halves(odd - even), weight(0, first))
        for where, y in ((evens, y_even), (odds, y_odd)):
            for i, p in enumerate(where):
                h_ref[p, :] = h_ref[p, :] + jnp.tanh(y[i * span : (i + 1) * span])

    for spot, row, lane in spots():
        h_ref[row, lane] = x_ref[spot, :]
    layer(0, 0)

    def section(s, _):
        for l in range(1, LAYERS):
            layer(s, l)
        for j in range(2, n):
            fetch(j, s).wait()
        u = jnp.tanh(dot3(halves(h_ref[...]), weight(2, s * width)) + tb_ref[s, 0:1, :])
        for g in range(groups):
            u_ref[g, :, :] = u[:, g * COLS : (g + 1) * COLS]
        mixed = dot3(halves(u), weight(6, 2 * s * width))

        frames = rows // MICS
        means = []
        for g in range(groups):
            total = u_ref[g, pl.ds(0, frames, stride=MICS), :]
            for m in range(1, MICS):
                total += u_ref[g, pl.ds(m, frames, stride=MICS), :]
            means.append(total * (1.0 / MICS))
        mean = jnp.concatenate(means, axis=1)
        v = jnp.tanh(dot3(halves(mean), weight(4, s * width)) + tb_ref[s, 1:2, :])
        pooled = dot3(halves(v), weight(6, 2 * s * width + width)) + tb_ref[s, 2:3, :]
        pooled = jnp.broadcast_to(pooled[:, None, :], (frames, MICS, width)).reshape(rows, width)
        h = h_ref[...] + jnp.tanh(mixed + pooled)
        h_ref[...] = h
        for spot, row, lane in spots():
            out_ref[spot, :] = h[row, lane]

        @pl.when(s < SECTIONS - 1)
        def _():
            layer(s + 1, 0)

        return 0

    lax.fori_loop(0, SECTIONS, section, 0)


def network(x, biases, weights):
    width = weights[0].shape[1]
    rows = x.size // width
    per = rows // MICS // 32
    scratch = [pltpu.VMEM((rows, width), F32), pltpu.VMEM((width // COLS, rows, COLS), F32)]
    scratch += [pltpu.VMEM(w.shape, w.dtype) for w in weights]
    scratch += [pltpu.SemaphoreType.DMA((len(weights), SECTIONS * LAYERS))]
    flops = 6 * rows * width * width * SECTIONS * (3 * LAYERS // 2 + 2)
    return pl.pallas_call(
        functools.partial(network_kernel, per),
        in_specs=[VMEM] * 3 + [ANY] * len(weights),
        out_specs=VMEM,
        out_shape=jax.ShapeDtypeStruct(x.shape, F32),
        scratch_shapes=scratch,
        compiler_params=PARAMS,
        cost_estimate=pl.CostEstimate(
            flops=flops, bytes_accessed=8 * x.size + sum(w.nbytes for w in weights), transcendentals=rows * width * 10
        ),
        name="network",
    )(x, *biases, *weights)


def exchange(pieces):
    return lax.all_to_all(pieces, BOTH, 0, 0, tiled=True)


def body(signal, conv_weight, conv_bias, transform_in, transform_mid, transform_out, transform_offsets_bias):
    frames, width = signal.shape[1:]
    devices = lax.axis_size(BOTH)
    held = frames // devices
    groups = width // COLS
    pieces = signal.reshape(held, devices, width).transpose(1, 0, 2)
    pieces = exchange(pieces)
    x = pieces.reshape(devices, held, groups, COLS).transpose(0, 2, 1, 3).reshape(-1, COLS)
    flat = [w.reshape(-1, width) for w in (transform_in, transform_mid, transform_out)]
    weights = [*split_taps(conv_weight.reshape(-1, width)), *split_dense(flat)]
    y = network(x, (conv_bias, transform_offsets_bias), weights)
    pieces = y.reshape(devices, groups, held, COLS).transpose(0, 2, 1, 3).reshape(devices, held, width)
    pieces = exchange(pieces)
    return pieces.transpose(1, 0, 2).reshape(signal.shape)


def solution(mesh):
    placed = (P("mic", "tm", None), P(), P(), P(), P(), P(), P())
    return jax.shard_map(body, mesh=mesh, in_specs=placed, out_specs=P("mic", "tm", None), check_vma=False)
```

time: 469 us -> 117 us (0.25); the launches traced: 459 us -> 117 us
  waiting for transfers between devices: 320 us -> 9.57 us
  matrix products: 94.6 us -> 0 us
  Pallas kernels: 0 us -> 52 us
  blocking collectives: 0 us -> 35 us
  starting transfers between devices: 28.7 us -> 11.9 us
  between operations: 14.1 us -> 0.03 us
  local copies, waits for them, and re-layouts: 2.33 us -> 7.88 us
    psum x2 -> x0, waiting for transfers between devices: 172 us -> none  [body(): summed = lax.psum(mapped, 'mic')]
    ppermute x6 -> x0, waiting for transfers between devices: 148 us -> none  [from_behind(): return lax.ppermute(x, axis, pairs)]
    dot_general x20 -> x0, matrix products: 94.6 us -> none  [matmul(): jnp.dot(left, right, precision=lax.Precision.HIGHEST, preferred_element_t...]
    pallas_call x0 -> x3, Pallas kernels: none -> 52 us  [the longest x1 32.7 us: network(): pl.pallas_call(functools.partial(network_kernel, per), in_specs=[VMEM] *...]
    all_to_all x0 -> x1, blocking collectives: none -> 35 us  [exchange(): return lax.all_to_all(pieces, BOTH, 0, 0, tiled=True)]
    ppermute x6 -> x0, starting transfers between devices: 28.2 us -> none  [from_behind(): return lax.ppermute(x, axis, pairs)]
    all_to_all x0 -> x1, starting transfers between devices: none -> 11.9 us  [exchange(): return lax.all_to_all(pieces, BOTH, 0, 0, tiled=True)]
    all_to_all x0 -> x1, waiting for transfers between devices: none -> 9.57 us  [exchange(): return lax.all_to_all(pieces, BOTH, 0, 0, tiled=True)]
  transfers between devices with their start and end apart: 8 -> 1, of which waited for: 8 -> 1; matrix products, arithmetic and copies ran while one was open for 7% -> 1% of each run, Pallas kernels for 0% -> 17%
where the time goes in v2:
time: 117 us
  Pallas kernels  52 us (44%)
  blocking collectives  35 us (30%)
  starting transfers between devices  11.9 us (10%)
  waiting for transfers between devices  9.57 us (8%)
  local copies, waits for them, and re-layouts  7.88 us (7%)
    all_to_all x1, blocking collectives, exchange(): return lax.all_to_all(pieces, BOTH, 0, 0, tiled=True)  35 us
    pallas_call x1, Pallas kernels, network(): pl.pallas_call(functools.partial(network_kernel, per), in_specs=[VMEM] *...  32.7 us
    pallas_call x1, Pallas kernels, split_taps(): pl.pallas_call(taps_kernel, grid=(layers,), in_specs=[pl.BlockSpec((rows...  12.2 us
    all_to_all x1, starting transfers between devices, exchange(): return lax.all_to_all(pieces, BOTH, 0, 0, tiled=True)  11.9 us
    all_to_all x1, waiting for transfers between devices, exchange(): return lax.all_to_all(pieces, BOTH, 0, 0, tiled=True)  9.57 us
    pallas_call x1, Pallas kernels, split_dense(): pl.pallas_call(dense_kernel, grid=(steps,), in_specs=specs, out_specs=[p...  7.14 us
    transpose x1, local copies, waits for them, and re-layouts, body(): pieces = signal.reshape(held, devices, width).transpose(1, 0, 2)  4.13 us
    transpose x1, local copies, waits for them, and re-layouts, body(): return pieces.transpose(1, 0, 2).reshape(signal.shape)  2.54 us
  transfers between devices with their start and end apart: 1, of which 1 were waited for; matrix products, arithmetic and copies ran while one was open for 1% of the time, Pallas kernels for 17%

profile of v2, /device:TPU:1, one launch (start us, length us, event | category | flops | bytes accessed | tf_op | source)
XLA Modules:
  0.0 116.5 jit_solution(5616159690246389302)
XLA Ops:
  0.0 4.1 %copy.16 = f32[128,8,512]{2,1,0:T(8,128)} copy(f32[128,8,512]{2,0,1:T(8,128)} %bitcast.22) | data formatting | bytes 4194304 | tf_op jit(solution)/shard_map/transpose | solution.py:203
  4.1 0.0 copy-start
  4.1 0.0 copy-start.1
  4.1 11.9 %all-to-all-start = ((f32[128,8,512]{2,1,0:T(8,128)}), f32[128,8,512]{2,1,0:T(8,128)}, u32[]{:S(2)}, u32[]{:S(2)}) async-start(f32[128,8,512]{2,1,0:T(8,128)} %copy.16), calls=%async_computation | async-start | bytes 4194304 | tf_op jit(solution)/shard_map/all_to_all | solution.py:195
  16.1 0.0 copy-done
  16.1 0.6 copy.17.cb_ref
  16.7 0.0 copy-done.1
  16.7 0.6 copy.18.tb_ref
  17.3 7.1 %split_dense.1 = (bf16[1024,512]{1,0:T(8,128)(2,1)}, bf16[1024,512]{1,0:T(8,128)(2,1)}, bf16[1024,512]{1,0:T(8,128)(2,1)}, bf16[1024,512]{1,0:T(8,128)(2,1)}, bf...) custom-call(f32[1024,512]{1,0:T(8,128)} %bitcast.24, f32[1024,512]{1,0:T(8,128)} %bitcast.25, f32[2048,512]{1,0:T(8,128)} %bitcast.21), custom_call_target="tpu_custom_call" | custom-call | flops 8388608 | bytes 16777216 | tf_op jit(solution)/shard_map/split_dense/pallas_call | solution.py:63
  24.5 12.2 %split_taps.1 = (bf16[9216,512]{1,0:T(8,128)(2,1)}, bf16[9216,512]{1,0:T(8,128)(2,1)}) custom-call(f32[6144,512]{1,0:T(8,128)} %bitcast.19), custom_call_target="tpu_custom_call" | custom-call | flops 18874368 | bytes 31457280 | tf_op jit(solution)/shard_map/split_taps/pallas_call | solution.py:42
  36.7 9.6 %all-to-all-done = f32[128,8,512]{2,1,0:T(8,128)} async-done(((f32[128,8,512]{2,1,0:T(8,128)}), f32[128,8,512]{2,1,0:T(8,128)}, u32[]{:S(2)}, u32[]{:S(2)}) %all-to-all-start) | async-done | bytes 2097184 | tf_op jit(solution)/shard_map/all_to_all | solution.py:195
  46.2 32.7 %network.1 = f32[4096,128]{1,0:T(8,128)} custom-call(f32[4096,128]{1,0:T(8,128)} %bitcast.4.x_ref, f32[2,3,512]{2,1,0:T(4,128)} %copy.17.cb_ref, f32[2,3,512]{2,1,0:T(4,128)} %copy.18.tb_ref, bf16[9216,512]{1,0:T(8,128)(2,1)} %get-tuple-element.13.refs_0_, bf16[9216,512]{1,0:T(8,128)(2,1)} %get-tuple-element.14.refs_1_, ...), custom_call_target="tpu_custom_call" | custom-call | flops 19327352832 | bytes 31457280 | tf_op jit(solution)/shard_map/network/pallas_call | solution.py:180
  78.9 35.0 %all_to_all.10 = f32[128,8,512]{2,1,0:T(8,128)S(1)} all-to-all(f32[128,8,512]{2,1,0:T(8,128)} %bitcast.23), channel_id=1, replica_groups=mesh['mic'=8,'tm'=16] {'mic','tm'}, dimensions={0} | all-to-all | bytes 4194304 | tf_op jit(solution)/shard_map/all_to_all | solution.py:195
  114.0 2.5 %copy.19 = f32[8,128,512]{2,1,0:T(8,128)} copy(f32[8,128,512]{2,0,1:T(8,128)S(1)} %bitcast.20) | data formatting | bytes 4194304 | tf_op jit(solution)/shard_map/transpose | solution.py:211
Async XLA Ops:
  4.1 12.0 %copy-start = (f32[2,3,512]{2,0,1:T(2,128)S(1)}, f32[2,3,512]{2,0,1:T(2,128)}, u32[]{:S(2)}) copy-start(f32[2,3,512]{2,0,1:T(2,128)} %param.9) | copy-start | bytes 36868
  4.1 12.6 %copy-start.1 = (f32[2,3,512]{2,0,1:T(2,128)S(1)}, f32[2,3,512]{2,0,1:T(2,128)}, u32[]{:S(2)}) copy-start(f32[2,3,512]{2,0,1:T(2,128)} %param.13) | copy-start | bytes 36868
  4.1 42.1 %all-to-all-start = ((f32[128,8,512]{2,1,0:T(8,128)}), f32[128,8,512]{2,1,0:T(8,128)}, u32[]{:S(2)}, u32[]{:S(2)}) async-start(f32[128,8,512]{2,1,0:T(8,128)} %copy.16), calls=%async_computation | async-start | bytes 4194304 | tf_op jit(solution)/shard_map/all_to_all | solution.py:195

commit v3 on v2

v3 whole, which is shorter than its diff:
```python
import functools

import jax
import jax.numpy as jnp
from jax import lax
from jax.experimental import pallas as pl
from jax.experimental.pallas import tpu as pltpu
from jax.sharding import PartitionSpec as P

SECTIONS = 2
LAYERS = 3
MICS = 8
TILE = 8
GRANT = 65400 * 1024
F32 = jnp.float32
BF16 = jnp.bfloat16
BOTH = ("mic", "tm")
VMEM = pl.BlockSpec(memory_space=pltpu.VMEM)
ANY = pl.BlockSpec(memory_space=pl.ANY)
PARAMS = pltpu.CompilerParams(vmem_limit_bytes=GRANT)


def halves(x):
    hi = x.astype(BF16)
    lo = (x - hi.astype(F32)).astype(BF16)
    return hi, lo


def taps_kernel(w_ref, hi_ref, lo_ref):
    width = w_ref.shape[1]
    now, past = w_ref[:width, :], w_ref[width:, :]
    for i, w in enumerate((now + past, now, past)):
        part = slice(i * width, (i + 1) * width)
        hi_ref[part, :], lo_ref[part, :] = halves(w)


def split_taps(w):
    layers = SECTIONS * LAYERS
    rows, width = w.shape
    spec = pl.BlockSpec((rows // layers // 2 * 3, width), lambda i: (i, 0))
    out = jax.ShapeDtypeStruct((rows // 2 * 3, width), BF16)
    return pl.pallas_call(
        taps_kernel,
        grid=(layers,),
        in_specs=[pl.BlockSpec((rows // layers, width), lambda i: (i, 0))],
        out_specs=[spec] * 2,
        out_shape=[out] * 2,
        compiler_params=PARAMS,
        cost_estimate=pl.CostEstimate(flops=6 * w.size, bytes_accessed=10 * w.size, transcendentals=0),
        name="split_taps",
    )(w)


def dense_kernel(*refs):
    n = len(refs) // 3
    for i in range(n):
        refs[n + 2 * i][...], refs[n + 2 * i + 1][...] = halves(refs[i][...])


def split_dense(arrays, steps=4):
    specs = [pl.BlockSpec((a.shape[0] // steps, a.shape[1]), lambda i: (i, 0)) for a in arrays]
    size = sum(a.size for a in arrays)
    return pl.pallas_call(
        dense_kernel,
        grid=(steps,),
        in_specs=specs,
        out_specs=[p for p in specs for _ in range(2)],
        out_shape=[jax.ShapeDtypeStruct(a.shape, BF16) for a in arrays for _ in range(2)],
        compiler_params=PARAMS,
        cost_estimate=pl.CostEstimate(flops=4 * size, bytes_accessed=8 * size, transcendentals=0),
        name="split_dense",
    )(*arrays)


def dot3(a, w):
    dot = functools.partial(jnp.dot, preferred_element_type=F32)
    return dot(a[0], w[0]) + dot(a[0], w[1]) + dot(a[1], w[0])


def network_kernel(x_ref, cb_ref, tb_ref, *refs):
    n = 8
    sources, h_ref = refs[:n], refs[n]
    held, sems = refs[n + 1 : 2 * n + 1], refs[2 * n + 1]
    rows, width = h_ref.shape
    frames = rows // MICS
    half = TILE // 2

    def fetch(j, k):
        size = width if j < 2 else held[j].shape[0] // SECTIONS
        part = pl.ds(pl.multiple_of(k * size, size), size)
        return pltpu.make_async_copy(sources[j].at[part, :], held[j].at[part, :], sems.at[j, k])

    for s in range(SECTIONS):
        for k in range(3 * LAYERS * s, 3 * LAYERS * (s + 1)):
            for j in range(2):
                fetch(j, k).start()
        for j in range(2, n):
            fetch(j, s).start()

    def weight(j, k):
        part = pl.ds(pl.multiple_of(k * width, width), width)
        return held[j][part, :], held[j + 1][part, :]

    top = lax.broadcasted_iota(jnp.int32, (rows // TILE // 2, TILE, width), 1) < half

    def swap(a):
        return pltpu.roll(a, half, axis=1)

    def pair(h, l):
        if l == 0:
            tiles = h.reshape(rows // TILE // 2, 2, TILE, width)
            a, b = tiles[:, 0], tiles[:, 1]
            even, odd = jnp.where(top, a, swap(b)), jnp.where(top, swap(a), b)
            turned = swap(odd).reshape(MICS, -1, TILE, width)
            before = jnp.concatenate([jnp.zeros((MICS, 1, TILE, width), F32), turned[:, :-1]], axis=1)
            past = jnp.where(top, before.reshape(odd.shape), turned.reshape(odd.shape))
        else:
            groups = h.reshape(MICS, -1, 2, half * 2**l, width)
            even, odd = groups[:, :, 0], groups[:, :, 1]
            past = jnp.concatenate([jnp.zeros_like(odd[:, :1]), odd[:, :-1]], axis=1)
        return [p.reshape(rows // 2, width) for p in (even, odd, past)]

    def join(even, odd, l):
        if l == 0:
            even, odd = (p.reshape(rows // TILE // 2, 1, TILE, width) for p in (even, odd))
            even, odd = even[:, 0], odd[:, 0]
            a, b = jnp.where(top, even, swap(odd)), jnp.where(top, swap(even), odd)
            both = jnp.concatenate([a[:, None], b[:, None]], axis=1)
        else:
            even, odd = (p.reshape(MICS, -1, 1, half * 2**l, width) for p in (even, odd))
            both = jnp.concatenate([even, odd], axis=2)
        return both.reshape(rows, width)

    def layer(h, s, l, eager):
        k = 3 * (s * LAYERS + l)

        def ready(*taps):
            for t in taps:
                for j in range(2):
                    fetch(j, k + t).wait()

        if not eager:
            ready(0, 1, 2)
        even, odd, past = pair(h, l)
        if eager:
            ready(0)
        shared = dot3(halves(even), weight(0, k)) + cb_ref[s, l : l + 1, :]
        if eager:
            ready(1, 2)
        y_odd = shared + dot3(halves(odd - even), weight(0, k + 1))
        y_even = shared + dot3(halves(past - even), weight(0, k + 2))
        h_ref[...] = join(even + jnp.tanh(y_even), odd + jnp.tanh(y_odd), l)

    layer(x_ref[...], 0, 0, True)

    def section(s, _):
        for l in range(1, LAYERS):
            layer(h_ref[...], s, l, False)
        for j in range(2, n):
            fetch(j, s).wait()
        u = jnp.tanh(dot3(halves(h_ref[...]), weight(2, s)) + tb_ref[s, 0:1, :])
        total = u[:frames]
        for m in range(1, MICS):
            total += u[m * frames : (m + 1) * frames]
        v = jnp.tanh(dot3(halves(total * (1.0 / MICS)), weight(4, s)) + tb_ref[s, 1:2, :])
        pooled = dot3(halves(v), weight(6, 2 * s + 1)) + tb_ref[s, 2:3, :]
        mixed = dot3(halves(u), weight(6, 2 * s))
        for m in range(MICS):
            part = slice(m * frames, (m + 1) * frames)
            h_ref[part, :] = h_ref[part, :] + jnp.tanh(mixed[part] + pooled)

        @pl.when(s < SECTIONS - 1)
        def _():
            layer(h_ref[...], s + 1, 0, False)

        return 0

    lax.fori_loop(0, SECTIONS, section, 0)


def network(x, biases, weights):
    rows, width = x.shape
    scratch = [pltpu.VMEM(w.shape, w.dtype) for w in weights]
    scratch += [pltpu.SemaphoreType.DMA((len(weights), 3 * SECTIONS * LAYERS))]
    flops = 6 * rows * width * width * SECTIONS * (3 * LAYERS // 2 + 2)
    return pl.pallas_call(
        network_kernel,
        in_specs=[VMEM] * 3 + [ANY] * len(weights),
        out_specs=VMEM,
        out_shape=jax.ShapeDtypeStruct(x.shape, F32),
        scratch_shapes=scratch,
        compiler_params=PARAMS,
        cost_estimate=pl.CostEstimate(
            flops=flops, bytes_accessed=8 * x.size + sum(w.nbytes for w in weights), transcendentals=rows * width * 10
        ),
        name="network",
    )(x, *biases, *weights)


def exchange(pieces):
    return lax.all_to_all(pieces, BOTH, 0, 0, tiled=True)


def body(signal, conv_weight, conv_bias, transform_in, transform_mid, transform_out, transform_offsets_bias):
    frames, width = signal.shape[1:]
    devices = lax.axis_size(BOTH)
    held = frames // devices
    pieces = signal.reshape(held, devices, width).transpose(1, 0, 2)
    pieces = exchange(pieces)
    flat = [w.reshape(-1, width) for w in (transform_in, transform_mid, transform_out)]
    weights = [*split_taps(conv_weight.reshape(-1, width)), *split_dense(flat)]
    y = network(pieces.reshape(frames, width), (conv_bias, transform_offsets_bias), weights)
    pieces = exchange(y.reshape(devices, held, width))
    return pieces.transpose(1, 0, 2).reshape(signal.shape)


def solution(mesh):
    placed = (P("mic", "tm", None), P(), P(), P(), P(), P(), P())
    return jax.shard_map(body, mesh=mesh, in_specs=placed, out_specs=P("mic", "tm", None), check_vma=False)
```

time: 117 us -> 115 us (0.983)
  Pallas kernels: 52 us -> 50.2 us
    reshape x0 -> x1, local copies, waits for them, and re-layouts: none -> 4.13 us  [body(): pieces = signal.reshape(held, devices, width).transpose(1, 0, 2)]
    transpose x1 -> x0, local copies, waits for them, and re-layouts: 4.13 us -> none  [body(): pieces = signal.reshape(held, devices, width).transpose(1, 0, 2)]
    pallas_call x1, Pallas kernels: 32.7 us -> 30.8 us  [network(): pl.pallas_call(network_kernel, in_specs=[VMEM] * 3 + [ANY] * len(weights)...]
where the time goes in v3:
time: 115 us
  Pallas kernels  50.2 us (44%)
  blocking collectives  35 us (30%)
  starting transfers between devices  11.9 us (10%)
  waiting for transfers between devices  9.53 us (8%)
  local copies, waits for them, and re-layouts  7.88 us (7%)
    all_to_all x1, blocking collectives, exchange(): return lax.all_to_all(pieces, BOTH, 0, 0, tiled=True)  35 us
    pallas_call x1, Pallas kernels, network(): pl.pallas_call(network_kernel, in_specs=[VMEM] * 3 + [ANY] * len(weights)...  30.8 us
    pallas_call x1, Pallas kernels, split_taps(): pl.pallas_call(taps_kernel, grid=(layers,), in_specs=[pl.BlockSpec((rows...  12.3 us
    all_to_all x1, starting transfers between devices, exchange(): return lax.all_to_all(pieces, BOTH, 0, 0, tiled=True)  11.9 us
    all_to_all x1, waiting for transfers between devices, exchange(): return lax.all_to_all(pieces, BOTH, 0, 0, tiled=True)  9.53 us
    pallas_call x1, Pallas kernels, split_dense(): pl.pallas_call(dense_kernel, grid=(steps,), in_specs=specs, out_specs=[p...  7.14 us
    reshape x1, local copies, waits for them, and re-layouts, body(): pieces = signal.reshape(held, devices, width).transpose(1, 0, 2)  4.13 us
    transpose x1, local copies, waits for them, and re-layouts, body(): return pieces.transpose(1, 0, 2).reshape(signal.shape)  2.54 us
  transfers between devices with their start and end apart: 1, of which 1 were waited for; matrix products, arithmetic and copies ran while one was open for 1% of the time, Pallas kernels for 17%

profile of v3, /device:TPU:1, one launch (start us, length us, event | category | flops | bytes accessed | tf_op | source)
XLA Modules:
  0.0 114.6 jit_solution(979129292037807899)
XLA Ops:
  0.0 4.1 %copy.13 = f32[8,128,512]{2,0,1:T(8,128)} copy(f32[8,128,512]{2,1,0:T(8,128)} %bitcast.15) | data formatting | bytes 4194304 | tf_op jit(solution)/shard_map/reshape | solution.py:208
  4.1 0.0 copy-start
  4.1 0.0 copy-start.1
  4.1 11.9 %all-to-all-start = ((f32[128,8,512]{2,1,0:T(8,128)}), f32[128,8,512]{2,1,0:T(8,128)}, u32[]{:S(2)}, u32[]{:S(2)}) async-start(f32[128,8,512]{2,1,0:T(8,128)} %bitcast.11), calls=%async_computation | async-start | bytes 4194304 | tf_op jit(solution)/shard_map/all_to_all | solution.py:201
  16.1 0.0 copy-done
  16.1 0.6 copy.9.cb_ref
  16.7 0.0 copy-done.1
  16.7 0.6 copy.10.tb_ref
  17.3 7.1 %split_dense.1 = (bf16[1024,512]{1,0:T(8,128)(2,1)}, bf16[1024,512]{1,0:T(8,128)(2,1)}, bf16[1024,512]{1,0:T(8,128)(2,1)}, bf16[1024,512]{1,0:T(8,128)(2,1)}, bf...) custom-call(f32[1024,512]{1,0:T(8,128)} %bitcast.17, f32[1024,512]{1,0:T(8,128)} %bitcast.18, f32[2048,512]{1,0:T(8,128)} %bitcast.14), custom_call_target="tpu_custom_call" | custom-call | flops 8388608 | bytes 16777216 | tf_op jit(solution)/shard_map/split_dense/pallas_call | solution.py:63
  24.5 12.3 %split_taps.1 = (bf16[9216,512]{1,0:T(8,128)(2,1)}, bf16[9216,512]{1,0:T(8,128)(2,1)}) custom-call(f32[6144,512]{1,0:T(8,128)} %bitcast.12), custom_call_target="tpu_custom_call" | custom-call | flops 18874368 | bytes 31457280 | tf_op jit(solution)/shard_map/split_taps/pallas_call | solution.py:42
  36.7 9.5 %all-to-all-done = f32[128,8,512]{2,1,0:T(8,128)} async-done(((f32[128,8,512]{2,1,0:T(8,128)}), f32[128,8,512]{2,1,0:T(8,128)}, u32[]{:S(2)}, u32[]{:S(2)}) %all-to-all-start) | async-done | bytes 2097184 | tf_op jit(solution)/shard_map/all_to_all | solution.py:201
  46.2 30.8 %network.1 = f32[1024,512]{1,0:T(8,128)} custom-call(f32[1024,512]{1,0:T(8,128)} %bitcast.2.x_ref, f32[2,3,512]{2,1,0:T(4,128)} %copy.9.cb_ref, f32[2,3,512]{2,1,0:T(4,128)} %copy.10.tb_ref, bf16[9216,512]{1,0:T(8,128)(2,1)} %get-tuple-element.13.refs_0_, bf16[9216,512]{1,0:T(8,128)(2,1)} %get-tuple-element.14.refs_1_, ...), custom_call_target="tpu_custom_call" | custom-call | flops 19327352832 | bytes 31457280 | tf_op jit(solution)/shard_map/network/pallas_call | solution.py:186
  77.1 35.0 %all_to_all.10 = f32[128,8,512]{2,1,0:T(8,128)S(1)} all-to-all(f32[128,8,512]{2,1,0:T(8,128)} %bitcast.16), channel_id=1, replica_groups=mesh['mic'=8,'tm'=16] {'mic','tm'}, dimensions={0} | all-to-all | bytes 4194304 | tf_op jit(solution)/shard_map/all_to_all | solution.py:201
  112.1 2.5 %copy.11 = f32[8,128,512]{2,1,0:T(8,128)} copy(f32[8,128,512]{2,0,1:T(8,128)S(1)} %bitcast.13) | data formatting | bytes 4194304 | tf_op jit(solution)/shard_map/transpose | solution.py:214
Async XLA Ops:
  4.1 12.0 %copy-start = (f32[2,3,512]{2,0,1:T(2,128)S(1)}, f32[2,3,512]{2,0,1:T(2,128)}, u32[]{:S(2)}) copy-start(f32[2,3,512]{2,0,1:T(2,128)} %param.9) | copy-start | bytes 36868
  4.1 12.6 %copy-start.1 = (f32[2,3,512]{2,0,1:T(2,128)S(1)}, f32[2,3,512]{2,0,1:T(2,128)}, u32[]{:S(2)}) copy-start(f32[2,3,512]{2,0,1:T(2,128)} %param.13) | copy-start | bytes 36868
  4.1 42.1 %all-to-all-start = ((f32[128,8,512]{2,1,0:T(8,128)}), f32[128,8,512]{2,1,0:T(8,128)}, u32[]{:S(2)}, u32[]{:S(2)}) async-start(f32[128,8,512]{2,1,0:T(8,128)} %bitcast.11), calls=%async_computation | async-start | bytes 4194304 | tf_op jit(solution)/shard_map/all_to_all | solution.py:201

commit v4 on v3

--- a/solution.py
+++ b/solution.py
@@ -11,7 +11,7 @@
 LAYERS = 3
 MICS = 8
 TILE = 8
-GRANT = 65400 * 1024
+GRANT = 59500 * 1024
 F32 = jnp.float32
 BF16 = jnp.bfloat16
 BOTH = ("mic", "tm")
@@ -51,21 +51,25 @@
     )(w)
 
 
-def dense_kernel(*refs):
-    n = len(refs) // 3
-    for i in range(n):
-        refs[n + 2 * i][...], refs[n + 2 * i + 1][...] = halves(refs[i][...])
-
-
-def split_dense(arrays, steps=4):
-    specs = [pl.BlockSpec((a.shape[0] // steps, a.shape[1]), lambda i: (i, 0)) for a in arrays]
+def dense_kernel(in_ref, mid_ref, out_ref, hi_ref, lo_ref):
+    first = 0
+    for ref in (in_ref, mid_ref, out_ref):
+        part = slice(first, first + ref.shape[0])
+        hi_ref[part, :], lo_ref[part, :] = halves(ref[...])
+        first += ref.shape[0]
+
+
+def split_dense(arrays, parts=2):
+    width = arrays[0].shape[1]
+    heights = [a.shape[0] // SECTIONS for a in arrays]
+    specs = [pl.BlockSpec((h, width // parts), lambda s, c: (s, c)) for h in heights + [sum(heights)] * 2]
     size = sum(a.size for a in arrays)
     return pl.pallas_call(
         dense_kernel,
-        grid=(steps,),
-        in_specs=specs,
-        out_specs=[p for p in specs for _ in range(2)],
-        out_shape=[jax.ShapeDtypeStruct(a.shape, BF16) for a in arrays for _ in range(2)],
+        grid=(SECTIONS, parts),
+        in_specs=specs[:-2],
+        out_specs=specs[-2:],
+        out_shape=[jax.ShapeDtypeStruct((SECTIONS * sum(heights), width), BF16)] * 2,
         compiler_params=PARAMS,
         cost_estimate=pl.CostEstimate(flops=4 * size, bytes_accessed=8 * size, transcendentals=0),
         name="split_dense",
@@ -78,7 +82,7 @@
 
 
 def network_kernel(x_ref, cb_ref, tb_ref, *refs):
-    n = 8
+    n = 4
     sources, h_ref = refs[:n], refs[n]
     held, sems = refs[n + 1 : 2 * n + 1], refs[2 * n + 1]
     rows, width = h_ref.shape
@@ -158,13 +162,13 @@
             layer(h_ref[...], s, l, False)
         for j in range(2, n):
             fetch(j, s).wait()
-        u = jnp.tanh(dot3(halves(h_ref[...]), weight(2, s)) + tb_ref[s, 0:1, :])
+        u = jnp.tanh(dot3(halves(h_ref[...]), weight(2, 4 * s)) + tb_ref[s, 0:1, :])
         total = u[:frames]
         for m in range(1, MICS):
             total += u[m * frames : (m + 1) * frames]
-        v = jnp.tanh(dot3(halves(total * (1.0 / MICS)), weight(4, s)) + tb_ref[s, 1:2, :])
-        pooled = dot3(halves(v), weight(6, 2 * s + 1)) + tb_ref[s, 2:3, :]
-        mixed = dot3(halves(u), weight(6, 2 * s))
+        v = jnp.tanh(dot3(halves(total * (1.0 / MICS)), weight(2, 4 * s + 1)) + tb_ref[s, 1:2, :])
+        pooled = dot3(halves(v), weight(2, 4 * s + 3)) + tb_ref[s, 2:3, :]
+        mixed = dot3(halves(u), weight(2, 4 * s + 2))
         for m in range(MICS):
             part = slice(m * frames, (m + 1) * frames)
             h_ref[part, :] = h_ref[part, :] + jnp.tanh(mixed[part] + pooled)
@@ -189,7 +193,7 @@
         out_specs=VMEM,
         out_shape=jax.ShapeDtypeStruct(x.shape, F32),
         scratch_shapes=scratch,
-        compiler_params=PARAMS,
+        compiler_params=pltpu.CompilerParams(vmem_limit_bytes=48 << 20),
         cost_estimate=pl.CostEstimate(
             flops=flops, bytes_accessed=8 * x.size + sum(w.nbytes for w in weights), transcendentals=rows * width * 10
         ),

time: 115 us -> 111 us (0.965)
  Pallas kernels: 50.2 us -> 46.9 us
  waiting for transfers between devices: 9.53 us -> 10.8 us
  local copies, waits for them, and re-layouts: 7.88 us -> 6.68 us
    pallas_call x1, Pallas kernels: 30.8 us -> 27.3 us  [network(): pl.pallas_call(network_kernel, in_specs=[VMEM] * 3 + [ANY] * len(weights)...]
    all_to_all x1, waiting for transfers between devices: 9.53 us -> 10.8 us  [exchange(): return lax.all_to_all(pieces, BOTH, 0, 0, tiled=True)]
    unnamed x6, local copies, waits for them, and re-layouts: 1.22 us -> 0.02 us
  transfers between devices with their start and end apart: 1 -> 1, of which waited for: 1 -> 1; matrix products, arithmetic and copies ran while one was open for 1% -> 0% of each run, Pallas kernels for 17% -> 18%
where the time goes in v4:
time: 111 us
  Pallas kernels  46.9 us (42%)
  blocking collectives  34.7 us (31%)
  starting transfers between devices  11.5 us (10%)
  waiting for transfers between devices  10.8 us (10%)
  local copies, waits for them, and re-layouts  6.68 us (6%)
    all_to_all x1, blocking collectives, exchange(): return lax.all_to_all(pieces, BOTH, 0, 0, tiled=True)  34.7 us
    pallas_call x1, Pallas kernels, network(): pl.pallas_call(network_kernel, in_specs=[VMEM] * 3 + [ANY] * len(weights)...  27.3 us
    pallas_call x1, Pallas kernels, split_taps(): pl.pallas_call(taps_kernel, grid=(layers,), in_specs=[pl.BlockSpec((rows...  12.2 us
    all_to_all x1, starting transfers between devices, exchange(): return lax.all_to_all(pieces, BOTH, 0, 0, tiled=True)  11.5 us
    all_to_all x1, waiting for transfers between devices, exchange(): return lax.all_to_all(pieces, BOTH, 0, 0, tiled=True)  10.8 us
    pallas_call x1, Pallas kernels, split_dense(): pl.pallas_call(dense_kernel, grid=(SECTIONS, parts), in_specs=specs[:-2],...  7.38 us
    reshape x1, local copies, waits for them, and re-layouts, body(): pieces = signal.reshape(held, devices, width).transpose(1, 0, 2)  4.13 us
    transpose x1, local copies, waits for them, and re-layouts, body(): return pieces.transpose(1, 0, 2).reshape(signal.shape)  2.54 us
  transfers between devices with their start and end apart: 1, of which 1 were waited for; matrix products, arithmetic and copies ran while one was open for 0% of the time, Pallas kernels for 18%

profile of v4, /device:TPU:1, one launch (start us, length us, event | category | flops | bytes accessed | tf_op | source)
XLA Modules:
  0.0 110.6 jit_solution(4229198753578409071)
XLA Ops:
  0.0 4.1 %copy.13 = f32[8,128,512]{2,0,1:T(8,128)} copy(f32[8,128,512]{2,1,0:T(8,128)} %bitcast.18) | data formatting | bytes 4194304 | tf_op jit(solution)/shard_map/reshape | solution.py:212
  4.1 0.0 copy-start
  4.1 0.0 copy-start.1
  4.1 11.5 %all-to-all-start = ((f32[128,8,512]{2,1,0:T(8,128)}), f32[128,8,512]{2,1,0:T(8,128)S(1)}, u32[]{:S(2)}, u32[]{:S(2)}) async-start(f32[128,8,512]{2,1,0:T(8,128)} %bitcast.15), calls=%async_computation | async-start | bytes 4194304 | tf_op jit(solution)/shard_map/all_to_all | solution.py:205
  15.6 0.0 copy-done
  15.6 0.0 copy-done.1
  15.7 7.4 %split_dense.1 = (bf16[4096,512]{1,0:T(8,128)(2,1)}, bf16[4096,512]{1,0:T(8,128)(2,1)}) custom-call(f32[1024,512]{1,0:T(8,128)} %bitcast.19, f32[1024,512]{1,0:T(8,128)} %bitcast.20, f32[2048,512]{1,0:T(8,128)} %bitcast.17), custom_call_target="tpu_custom_call" | custom-call | flops 8388608 | bytes 16777216 | tf_op jit(solution)/shard_map/split_dense/pallas_call | solution.py:67
  23.0 12.2 %split_taps.1 = (bf16[9216,512]{1,0:T(8,128)(2,1)}, bf16[9216,512]{1,0:T(8,128)(2,1)}) custom-call(f32[6144,512]{1,0:T(8,128)} %bitcast.14), custom_call_target="tpu_custom_call" | custom-call | flops 18874368 | bytes 31457280 | tf_op jit(solution)/shard_map/split_taps/pallas_call | solution.py:42
  35.3 10.8 %all-to-all-done = f32[128,8,512]{2,1,0:T(8,128)S(1)} async-done(((f32[128,8,512]{2,1,0:T(8,128)}), f32[128,8,512]{2,1,0:T(8,128)S(1)}, u32[]{:S(2)}, u32[]{:S(2)}) %all-to-all-start) | async-done | bytes 2097184 | tf_op jit(solution)/shard_map/all_to_all | solution.py:205
  46.1 27.3 %network.1 = f32[1024,512]{1,0:T(8,128)S(1)} custom-call(f32[1024,512]{1,0:T(8,128)S(1)} %bitcast.12, f32[2,3,512]{2,1,0:T(4,128)S(1)} %copy.9.cb_ref, f32[2,3,512]{2,1,0:T(4,128)S(1)} %copy.10.tb_ref, bf16[9216,512]{1,0:T(8,128)(2,1)} %get-tuple-element.9.refs_0_, bf16[9216,512]{1,0:T(8,128)(2,1)} %get-tuple-element.10.refs_1_, ...), custom_call_target="tpu_custom_call" | custom-call | flops 19327352832 | bytes 31457280 | tf_op jit(solution)/shard_map/network/pallas_call | solution.py:190
  73.4 34.7 %all_to_all.10 = f32[128,8,512]{2,1,0:T(8,128)S(1)} all-to-all(f32[128,8,512]{2,1,0:T(8,128)S(1)} %bitcast.13), channel_id=1, replica_groups=mesh['mic'=8,'tm'=16] {'mic','tm'}, dimensions={0} | all-to-all | bytes 4194304 | tf_op jit(solution)/shard_map/all_to_all | solution.py:205
  108.1 2.5 %copy.11 = f32[8,128,512]{2,1,0:T(8,128)} copy(f32[8,128,512]{2,0,1:T(8,128)S(1)} %bitcast.16) | data formatting | bytes 4194304 | tf_op jit(solution)/shard_map/transpose | solution.py:218
  (2 shorter events, 0.0 us)
Async XLA Ops:
  4.1 11.5 %copy-start = (f32[2,3,512]{2,0,1:T(2,128)S(1)}, f32[2,3,512]{2,0,1:T(2,128)}, u32[]{:S(2)}) copy-start(f32[2,3,512]{2,0,1:T(2,128)} %param.9) | copy-start | bytes 36868
  4.1 11.5 %copy-start.1 = (f32[2,3,512]{2,0,1:T(2,128)S(1)}, f32[2,3,512]{2,0,1:T(2,128)}, u32[]{:S(2)}) copy-start(f32[2,3,512]{2,0,1:T(2,128)} %param.13) | copy-start | bytes 36868
  4.1 42.0 %all-to-all-start = ((f32[128,8,512]{2,1,0:T(8,128)}), f32[128,8,512]{2,1,0:T(8,128)S(1)}, u32[]{:S(2)}, u32[]{:S(2)}) async-start(f32[128,8,512]{2,1,0:T(8,128)} %bitcast.15), calls=%async_computation | async-start | bytes 4194304 | tf_op jit(solution)/shard_map/all_to_all | solution.py:205

commit v5 on v4

--- a/solution.py
+++ b/solution.py
@@ -163,12 +163,12 @@
         for j in range(2, n):
             fetch(j, s).wait()
         u = jnp.tanh(dot3(halves(h_ref[...]), weight(2, 4 * s)) + tb_ref[s, 0:1, :])
+        mixed = dot3(halves(u), weight(2, 4 * s + 2))
         total = u[:frames]
         for m in range(1, MICS):
             total += u[m * frames : (m + 1) * frames]
         v = jnp.tanh(dot3(halves(total * (1.0 / MICS)), weight(2, 4 * s + 1)) + tb_ref[s, 1:2, :])
         pooled = dot3(halves(v), weight(2, 4 * s + 3)) + tb_ref[s, 2:3, :]
-        mixed = dot3(halves(u), weight(2, 4 * s + 2))
         for m in range(MICS):
             part = slice(m * frames, (m + 1) * frames)
             h_ref[part, :] = h_ref[part, :] + jnp.tanh(mixed[part] + pooled)

time: 111 us -> 111 us (level)
  no operation moved by 1% of the time
where the time goes in v5:
time: 111 us
  Pallas kernels  47.3 us (43%)
  blocking collectives  34.7 us (31%)
  starting transfers between devices  11.5 us (10%)
  waiting for transfers between devices  10.8 us (10%)
  local copies, waits for them, and re-layouts  6.68 us (6%)
    all_to_all x1, blocking collectives, exchange(): return lax.all_to_all(pieces, BOTH, 0, 0, tiled=True)  34.7 us
    pallas_call x1, Pallas kernels, network(): pl.pallas_call(network_kernel, in_specs=[VMEM] * 3 + [ANY] * len(weights)...  27.7 us
    pallas_call x1, Pallas kernels, split_taps(): pl.pallas_call(taps_kernel, grid=(layers,), in_specs=[pl.BlockSpec((rows...  12.2 us
    all_to_all x1, starting transfers between devices, exchange(): return lax.all_to_all(pieces, BOTH, 0, 0, tiled=True)  11.5 us
    all_to_all x1, waiting for transfers between devices, exchange(): return lax.all_to_all(pieces, BOTH, 0, 0, tiled=True)  10.8 us
    pallas_call x1, Pallas kernels, split_dense(): pl.pallas_call(dense_kernel, grid=(SECTIONS, parts), in_specs=specs[:-2],...  7.38 us
    reshape x1, local copies, waits for them, and re-layouts, body(): pieces = signal.reshape(held, devices, width).transpose(1, 0, 2)  4.13 us
    transpose x1, local copies, waits for them, and re-layouts, body(): return pieces.transpose(1, 0, 2).reshape(signal.shape)  2.54 us
  transfers between devices with their start and end apart: 1, of which 1 were waited for; matrix products, arithmetic and copies ran while one was open for 0% of the time, Pallas kernels for 18%

profile of v5, /device:TPU:1, one launch (start us, length us, event | category | flops | bytes accessed | tf_op | source)
XLA Modules:
  0.0 111.1 jit_solution(947420906704630493)
XLA Ops:
  0.0 4.1 %copy.13 = f32[8,128,512]{2,0,1:T(8,128)} copy(f32[8,128,512]{2,1,0:T(8,128)} %bitcast.18) | data formatting | bytes 4194304 | tf_op jit(solution)/shard_map/reshape | solution.py:212
  4.1 0.0 copy-start
  4.1 0.0 copy-start.1
  4.1 11.5 %all-to-all-start = ((f32[128,8,512]{2,1,0:T(8,128)}), f32[128,8,512]{2,1,0:T(8,128)S(1)}, u32[]{:S(2)}, u32[]{:S(2)}) async-start(f32[128,8,512]{2,1,0:T(8,128)} %bitcast.15), calls=%async_computation | async-start | bytes 4194304 | tf_op jit(solution)/shard_map/all_to_all | solution.py:205
  15.6 0.0 copy-done
  15.6 0.0 copy-done.1
  15.7 7.4 %split_dense.1 = (bf16[4096,512]{1,0:T(8,128)(2,1)}, bf16[4096,512]{1,0:T(8,128)(2,1)}) custom-call(f32[1024,512]{1,0:T(8,128)} %bitcast.19, f32[1024,512]{1,0:T(8,128)} %bitcast.20, f32[2048,512]{1,0:T(8,128)} %bitcast.17), custom_call_target="tpu_custom_call" | custom-call | flops 8388608 | bytes 16777216 | tf_op jit(solution)/shard_map/split_dense/pallas_call | solution.py:67
  23.0 12.2 %split_taps.1 = (bf16[9216,512]{1,0:T(8,128)(2,1)}, bf16[9216,512]{1,0:T(8,128)(2,1)}) custom-call(f32[6144,512]{1,0:T(8,128)} %bitcast.14), custom_call_target="tpu_custom_call" | custom-call | flops 18874368 | bytes 31457280 | tf_op jit(solution)/shard_map/split_taps/pallas_call | solution.py:42
  35.3 10.8 %all-to-all-done = f32[128,8,512]{2,1,0:T(8,128)S(1)} async-done(((f32[128,8,512]{2,1,0:T(8,128)}), f32[128,8,512]{2,1,0:T(8,128)S(1)}, u32[]{:S(2)}, u32[]{:S(2)}) %all-to-all-start) | async-done | bytes 2097184 | tf_op jit(solution)/shard_map/all_to_all | solution.py:205
  46.1 27.7 %network.1 = f32[1024,512]{1,0:T(8,128)S(1)} custom-call(f32[1024,512]{1,0:T(8,128)S(1)} %bitcast.12, f32[2,3,512]{2,1,0:T(4,128)S(1)} %copy.9.cb_ref, f32[2,3,512]{2,1,0:T(4,128)S(1)} %copy.10.tb_ref, bf16[9216,512]{1,0:T(8,128)(2,1)} %get-tuple-element.9.refs_0_, bf16[9216,512]{1,0:T(8,128)(2,1)} %get-tuple-element.10.refs_1_, ...), custom_call_target="tpu_custom_call" | custom-call | flops 19327352832 | bytes 31457280 | tf_op jit(solution)/shard_map/network/pallas_call | solution.py:190
  73.9 34.7 %all_to_all.10 = f32[128,8,512]{2,1,0:T(8,128)S(1)} all-to-all(f32[128,8,512]{2,1,0:T(8,128)S(1)} %bitcast.13), channel_id=1, replica_groups=mesh['mic'=8,'tm'=16] {'mic','tm'}, dimensions={0} | all-to-all | bytes 4194304 | tf_op jit(solution)/shard_map/all_to_all | solution.py:205
  108.6 2.5 %copy.11 = f32[8,128,512]{2,1,0:T(8,128)} copy(f32[8,128,512]{2,0,1:T(8,128)S(1)} %bitcast.16) | data formatting | bytes 4194304 | tf_op jit(solution)/shard_map/transpose | solution.py:218
  (2 shorter events, 0.0 us)
Async XLA Ops:
  4.1 11.5 %copy-start = (f32[2,3,512]{2,0,1:T(2,128)S(1)}, f32[2,3,512]{2,0,1:T(2,128)}, u32[]{:S(2)}) copy-start(f32[2,3,512]{2,0,1:T(2,128)} %param.9) | copy-start | bytes 36868
  4.1 11.5 %copy-start.1 = (f32[2,3,512]{2,0,1:T(2,128)S(1)}, f32[2,3,512]{2,0,1:T(2,128)}, u32[]{:S(2)}) copy-start(f32[2,3,512]{2,0,1:T(2,128)} %param.13) | copy-start | bytes 36868
  4.1 42.0 %all-to-all-start = ((f32[128,8,512]{2,1,0:T(8,128)}), f32[128,8,512]{2,1,0:T(8,128)S(1)}, u32[]{:S(2)}, u32[]{:S(2)}) async-start(f32[128,8,512]{2,1,0:T(8,128)} %bitcast.15), calls=%async_computation | async-start | bytes 4194304 | tf_op jit(solution)/shard_map/all_to_all | solution.py:205
